TPU v7x, 512 devices: a whole 4x8x8 slice. The times are simulated.
512 devices in a mesh: crate: 32 (over z, x), board: 16 (over y, core).
Axes of the slice: x: 4, y: 8, z: 8, core: 2. Of those that a mesh axis runs over, the one named last changes fastest.
Arguments:
- voltages: bfloat16 [2048, 65536], P(('crate', 'board')), may hold values from -6 to 6
- wiring: int32 [2048], replicated, may hold values from 0 to 2047, each once
- positions: float32 [2, 2048], replicated, may hold values from -4 to 4
- directions: float32 [2, 512], replicated, may hold values from -1 to 1
- gains: float32 [2, 256, 2048], P(None, 'crate'), may hold values from -6 to 6
- delays: int32 [256, 512], replicated, may hold values from 0 to 31
Outputs:
- dedispersed: float32 [512, 512, 32], P('crate', 'board')
Inputs may be any that keep to these rules, and one draw needn't show every extreme that they name: `wiring`: each of the 2048 antennas is wired to exactly one input row.
All inputs are finite; a program needn't handle non-finite values.
Results may differ from a plain program's by a relative error of at most 0.0096.
Values may be sent and summed in bfloat16 or wider, within the bound.
A program may use at most 64 MiB of HBM per device.

v0:
```python
import math

import jax
import jax.numpy as jnp
from jax import lax
from jax.sharding import PartitionSpec as P

ANTENNA_INPUTS = 2048
FREQ_CHANNELS = 256
FRAME_SAMPLES = 512
BEAMS = 512
DMS = 512
SPECTRUM_BATCHES = 2
BATCH_SPECTRA = 64
AVG = 4
BINS = 16
TB = 32


two_pi = 2.0 * math.pi


def filter_table():
    sample_ids = jnp.arange(FRAME_SAMPLES, dtype=jnp.int32)
    column_ids = jnp.arange(FREQ_CHANNELS, dtype=jnp.int32)
    window = 0.5 - 0.5 * jnp.cos(two_pi / FRAME_SAMPLES * sample_ids.astype(jnp.float32))
    turn_ids = sample_ids[:, None] * column_ids[None, :] % FRAME_SAMPLES
    phase_angle = two_pi / FRAME_SAMPLES * turn_ids.astype(jnp.float32)
    scale_norm_factor = 1.0 / math.sqrt(3.0 * FRAME_SAMPLES / 8.0)
    real_part = window[:, None] * jnp.cos(phase_angle) * scale_norm_factor
    imag_part = -window[:, None] * jnp.sin(phase_angle) * scale_norm_factor
    return jnp.concatenate([real_part, imag_part], axis=1).astype(jnp.bfloat16)


def beam_weights(channel, directions, place_x, place_y, gain_re, gain_im):
    geo_delay = (
        directions[0][:, None] * place_x[None, :] + directions[1][:, None] * place_y[None, :]
    )
    factor = two_pi * (1.0 + channel.astype(jnp.float32) / FREQ_CHANNELS)
    phase_angle = factor * geo_delay
    cosine = jnp.cos(phase_angle)
    sine_value = jnp.sin(phase_angle)
    scale_norm_factor = 1.0 / math.sqrt(ANTENNA_INPUTS)
    weight_re = (
        (gain_re[None, :] * cosine + gain_im[None, :] * sine_value) * scale_norm_factor
    ).astype(jnp.bfloat16)
    weight_im = (
        (gain_im[None, :] * cosine - gain_re[None, :] * sine_value) * scale_norm_factor
    ).astype(jnp.bfloat16)
    return (weight_re, weight_im)


def dedisperse(series, delay_table):
    bin_count = series.shape[2]
    bin_ids = jnp.arange(bin_count, dtype=jnp.int32)
    turn_ids = bin_ids[:, None] * bin_ids[None, :] % bin_count
    phase_angle = two_pi / bin_count * turn_ids.astype(jnp.float32)
    cos_table = jnp.cos(phase_angle)
    sin_table = jnp.sin(phase_angle)
    spec_re = jnp.einsum("bct,tk->kcb", series, cos_table, precision=lax.Precision.HIGHEST)
    spec_im = -jnp.einsum("bct,tk->kcb", series, sin_table, precision=lax.Precision.HIGHEST)

    def per_freq(inputs):
        freq_id, part_re, part_im = inputs
        shift_angle = two_pi / bin_count * (freq_id * delay_table % bin_count).astype(jnp.float32)
        shift_re = jnp.cos(shift_angle)
        shift_im = jnp.sin(shift_angle)
        out_re = jnp.einsum(
            "cd,cb->db", shift_re, part_re, precision=lax.Precision.HIGHEST
        ) - jnp.einsum("cd,cb->db", shift_im, part_im, precision=lax.Precision.HIGHEST)
        out_im = jnp.einsum(
            "cd,cb->db", shift_re, part_im, precision=lax.Precision.HIGHEST
        ) + jnp.einsum("cd,cb->db", shift_im, part_re, precision=lax.Precision.HIGHEST)
        return (out_re, out_im)

    freq_re, freq_im = lax.map(per_freq, (bin_ids, spec_re, spec_im))
    keep_mask = (bin_ids > 0).astype(jnp.float32)[:, None]
    scale_norm_factor = 1.0 / (bin_count * math.sqrt(FREQ_CHANNELS))
    first_term = jnp.einsum(
        "kdb,kt->bdt", freq_re, cos_table * keep_mask, precision=lax.Precision.HIGHEST
    )
    second_term = jnp.einsum(
        "kdb,kt->bdt", freq_im, sin_table * keep_mask, precision=lax.Precision.HIGHEST
    )
    return (first_term - second_term) * scale_norm_factor


def shards(voltages, wiring, positions, directions, gains, delays):
    crate_list = lax.axis_size("crate")
    board_list = lax.axis_size("board")
    crate_index = lax.axis_index("crate")
    board_index = lax.axis_index("board")
    local_antenna = voltages.shape[0]
    channel_groups = SPECTRUM_BATCHES * FREQ_CHANNELS // (crate_list * board_list)
    dft_table = filter_table()
    sample_frames = voltages.reshape(
        local_antenna * SPECTRUM_BATCHES * BATCH_SPECTRA, FRAME_SAMPLES
    )
    spectrum_rows = jnp.dot(sample_frames, dft_table, preferred_element_type=jnp.float32).astype(
        jnp.bfloat16
    )
    spectrum_rows = spectrum_rows.reshape(
        local_antenna, SPECTRUM_BATCHES, BATCH_SPECTRA, 2, FREQ_CHANNELS
    ).transpose(4, 1, 0, 3, 2)
    spectrum_rows = spectrum_rows.reshape(
        crate_list, board_list, channel_groups, local_antenna, 2 * BATCH_SPECTRA
    )
    position_grid = jnp.arange(ANTENNA_INPUTS, dtype=jnp.int32).reshape(
        crate_list, board_list, local_antenna
    )
    received_data = lax.all_to_all(
        lax.all_to_all(spectrum_rows, "crate", split_axis=0, concat_axis=3, tiled=True),
        "board",
        split_axis=1,
        concat_axis=3,
        tiled=True,
    )
    position_ids = position_grid.transpose(1, 0, 2).reshape(ANTENNA_INPUTS)
    received_data = received_data.reshape(channel_groups, ANTENNA_INPUTS, 2 * BATCH_SPECTRA)
    antenna = jnp.take(wiring, position_ids)
    place_x = jnp.take(positions[0], antenna)
    place_y = jnp.take(positions[1], antenna)
    gains_slot = jnp.take(gains, antenna, axis=2)
    gain_rows = gains.shape[1]
    first_group = (crate_index * board_list + board_index) * channel_groups
    beam_block = 256
    block_count = BEAMS // beam_block
    dir_blocks = directions.reshape(2, block_count, beam_block).transpose(1, 0, 2)

    def group_power(inputs):
        group_id, columns = inputs
        whole_id = first_group + group_id
        channel = whole_id // SPECTRUM_BATCHES
        gain_row = channel - crate_index * gain_rows
        gain_re = lax.dynamic_index_in_dim(gains_slot[0], gain_row, 0, keepdims=False)
        gain_im = lax.dynamic_index_in_dim(gains_slot[1], gain_row, 0, keepdims=False)

        def block_power(dir_block):
            weight_re, weight_im = beam_weights(
                channel, dir_block, place_x, place_y, gain_re, gain_im
            )
            real_side = jnp.dot(weight_re, columns, preferred_element_type=jnp.float32)
            imag_side = jnp.dot(weight_im, columns, preferred_element_type=jnp.float32)
            beam_re = real_side[:, :BATCH_SPECTRA] - imag_side[:, BATCH_SPECTRA:]
            beam_im = real_side[:, BATCH_SPECTRA:] + imag_side[:, :BATCH_SPECTRA]
            beam_power = (
                (beam_re * beam_re + beam_im * beam_im).reshape(beam_block, BINS, AVG).mean(axis=2)
            )
            return beam_power.astype(jnp.bfloat16)

        return lax.map(block_power, dir_blocks).reshape(BEAMS, BINS)

    powers = lax.map(group_power, (jnp.arange(channel_groups, dtype=jnp.int32), received_data))
    beam_local = BEAMS // crate_list
    dm_local = DMS // board_list
    dm_delays = lax.dynamic_slice_in_dim(delays, board_index * dm_local, dm_local, 1)
    regrouped = lax.all_to_all(powers, "crate", split_axis=1, concat_axis=0, tiled=True)
    empty_table = jnp.zeros((SPECTRUM_BATCHES * FREQ_CHANNELS, beam_local, BINS), jnp.bfloat16)
    portion = lax.all_gather(regrouped, "board", axis=0, tiled=True)
    row_count = portion.shape[0]
    row_ids = jnp.arange(row_count, dtype=jnp.int32)
    source_board = row_ids // (crate_list * channel_groups)
    source_crate = row_ids // channel_groups % crate_list
    whole_ids = (
        source_crate * board_list + source_board
    ) * channel_groups + row_ids % channel_groups
    table = empty_table.at[whole_ids].set(portion)
    series = (
        table.reshape(FREQ_CHANNELS, SPECTRUM_BATCHES, beam_local, BINS)
        .transpose(2, 0, 1, 3)
        .reshape(beam_local, FREQ_CHANNELS, TB)
        .astype(jnp.float32)
    )
    result = dedisperse(series, dm_delays)
    return result


def solution(mesh):
    in_specs = (P(("crate", "board"), None), P(), P(), P(), P(None, "crate", None), P())
    out_specs = P("crate", "board", None)
    return jax.shard_map(shards, mesh=mesh, in_specs=in_specs, out_specs=out_specs, check_vma=False)
```

profile of v0, /device:TPU:1, one launch (start us, length us, event | category | flops | bytes accessed | tf_op | source)
XLA Modules:
  0.0 482.1 jit_solution(1558080321978159391)
XLA Ops:
  0.1 1.5 reshape.310
  1.6 2.3 multiply_convert_fusion.5
  7.0 13.7 %all-to-all-start = ((bf16[32,16,1,4,128]{4,1,3,2,0:T(8,128)(2,1)}), bf16[32,16,1,4,128]{4,1,3,2,0:T(8,128)(2,1)S(1)}, u32[]{:S(2)}, u32[]{:S(2)}) async-start(bf16[32,16,1,4,128]{4,1,3,2,0:T(8,128)(2,1)} %copy.49), calls=%async_computation | async-start | bytes 1048576 | tf_op jit(solution)/shard_map/all_to_all | solution.py:112
  21.2 11.8 %gather_fusion = s32[2048]{0:T(1024)S(1)} fusion(s32[2048]{0:T(1024)S(1)} %copy-done.1, s32[2048]{0:T(1024)S(1)} %broadcast_clamp_fusion.2), kind=kCustom, calls=%fused_computation.2 | custom fusion | bytes 24576 | tf_op jit(solution)/shard_map/jit(_take)/gather | solution.py:120
  34.1 11.8 %gather_fusion.3 = f32[2048]{0:T(1024)S(1)} fusion(f32[2048]{0:T(1024)S(1)} %bitcast.105, s32[2048]{0:T(1024)S(1)} %broadcast_clamp_fusion), kind=kCustom, calls=%fused_computation.1.clone | custom fusion | bytes 24576 | tf_op jit(solution)/shard_map/jit(_take)/gather | solution.py:122
  45.9 11.8 %gather_fusion.2 = f32[2048]{0:T(1024)S(1)} fusion(f32[2048]{0:T(1024)S(1)} %bitcast.104, s32[2048]{0:T(1024)S(1)} %broadcast_clamp_fusion), kind=kCustom, calls=%fused_computation.clone | custom fusion | bytes 24576 | tf_op jit(solution)/shard_map/jit(_take)/gather | solution.py:121
  57.7 14.5 %gather_fusion.1 = f32[2048,2,8]{2,1,0:T(2,128)} fusion(f32[2,8,2048]{1,0,2:T(2,128)S(1)} %copy.46, s32[2048]{0:T(1024)S(1)} %broadcast_clamp_fusion.1), kind=kCustom, calls=%fused_computation.3 | custom fusion | bytes 270336 | tf_op jit(solution)/shard_map/jit(_take)/gather | solution.py:123
  72.2 10.0 %select_bitcast_fusion = f32[2,8,2048]{1,0,2:T(2,128)S(1)} fusion(f32[2048,2,8]{2,1,0:T(2,128)} %gather_fusion.1, pred[2048]{0:T(1024)(128)(4,1)S(1)} %get-tuple-element.303), kind=kLoop, calls=%fused_computation.56 | loop fusion | flops 32768 | bytes 264192 | tf_op jit(solution)/shard_map/jit(_take)/select_n | solution.py:123
  83.1 8.6 %all-to-all-start.1 = ((bf16[1,16,1,128,128]{4,3,2,0,1:T(8,128)(2,1)}), bf16[1,16,1,128,128]{4,3,2,0,1:T(8,128)(2,1)}, u32[]{:S(2)}, u32[]{:S(2)}) async-start(bf16[1,16,1,128,128]{4,3,2,0,1:T(8,128)(2,1)} %copy.50), calls=%async_computation.1 | async-start | bytes 1048576 | tf_op jit(solution)/shard_map/all_to_all | solution.py:111
  91.9 1.7 fusion.92
  93.5 57.0 %dynamic-slice_reduce_fusion = (f32[2048]{0:T(1024)S(1)}, f32[2048]{0:T(1024)S(1)}) fusion(f32[1,8,2048]{1,0,2:T(1,128)S(1)} %get-tuple-element.308, s32[]{:T(128)S(6)} %select_n.164, f32[1,8,2048]{1,0,2:T(1,128)S(1)} %get-tuple-element.309), kind=kLoop, calls=%fused_computation.65 | loop fusion | bytes 32772 | tf_op jit(solution)/shard_map/while/body/eval_jaxpr/jit(dynamic_index_in_dim)/dynamic_slice | solution.py:136
  150.6 48.7 %while.33 = (s32[]{:T(128)}, bf16[2,256,16]{1,2,0:T(8,128)(2,1)S(1)}, f32[2048]{0:T(1024)S(1)}, f32[]{:T(128)}, f32[2,2,256]{2,1,0:T(2,128)S(1)}, /*index=5*/f32...) while((s32[]{:T(128)}, ...), condition=%wide.region_2.4_spmd, body=%wide.region_0.3_spmd.sunk | while | flops 277975040 | bytes 1949857 | solution.py:151
  162.4 9.1 %fusion.116 = f32[256,128]{0,1:T(8,128)S(1)} fusion(bf16[2048,128]{1,0:T(8,128)(2,1)} %get-tuple-element.456, f32[2048]{0:T(1024)S(1)} %get-tuple-element.455, f32[2048]{0:T(1024)S(1)} %get-tuple-element.454, f32[256]{0:T(256)S(1)} %bitcast.120, f32[2048]{0:T(1024)S(1)} %get-tuple-element.453, f32[256]{0:T(256)S(1)} %bitcast.118, ...), kind=kOutput, calls=%fused_computation.10.clone.1 | convolution fusion | flops 138936320 | bytes 690180 | tf_op jit(solution)/shard_map/while/body/eval_jaxpr/while/body/eval_jaxpr/dot_general | solution.py:142
  171.5 9.1 %fusion.115 = f32[256,128]{0,1:T(8,128)S(1)} fusion(bf16[2048,128]{1,0:T(8,128)(2,1)} %get-tuple-element.456, f32[2048]{0:T(1024)S(1)} %get-tuple-element.455, f32[2048]{0:T(1024)S(1)} %get-tuple-element.454, f32[256]{0:T(256)S(1)} %bitcast.121, f32[2048]{0:T(1024)S(1)} %get-tuple-element.453, f32[256]{0:T(256)S(1)} %bitcast.119, ...), kind=kOutput, calls=%fused_computation.11.clone.1 | convolution fusion | flops 138936320 | bytes 690180 | tf_op jit(solution)/shard_map/while/body/eval_jaxpr/while/body/eval_jaxpr/dot_general | solution.py:143
  180.8 9.1 %fusion.116 = f32[256,128]{0,1:T(8,128)S(1)} fusion(bf16[2048,128]{1,0:T(8,128)(2,1)} %get-tuple-element.456, f32[2048]{0:T(1024)S(1)} %get-tuple-element.455, f32[2048]{0:T(1024)S(1)} %get-tuple-element.454, f32[256]{0:T(256)S(1)} %bitcast.120, f32[2048]{0:T(1024)S(1)} %get-tuple-element.453, f32[256]{0:T(256)S(1)} %bitcast.118, ...), kind=kOutput, calls=%fused_computation.10.clone.1 | convolution fusion | flops 138936320 | bytes 690180 | tf_op jit(solution)/shard_map/while/body/eval_jaxpr/while/body/eval_jaxpr/dot_general | solution.py:142
  189.9 9.1 %fusion.115 = f32[256,128]{0,1:T(8,128)S(1)} fusion(bf16[2048,128]{1,0:T(8,128)(2,1)} %get-tuple-element.456, f32[2048]{0:T(1024)S(1)} %get-tuple-element.455, f32[2048]{0:T(1024)S(1)} %get-tuple-element.454, f32[256]{0:T(256)S(1)} %bitcast.121, f32[2048]{0:T(1024)S(1)} %get-tuple-element.453, f32[256]{0:T(256)S(1)} %bitcast.119, ...), kind=kOutput, calls=%fused_computation.11.clone.1 | convolution fusion | flops 138936320 | bytes 690180 | tf_op jit(solution)/shard_map/while/body/eval_jaxpr/while/body/eval_jaxpr/dot_general | solution.py:143
  200.0 1.4 reduce.4
  202.2 9.5 %all-to-all-start.2 = ((bf16[32,2,128]{2,1,0:T(2,128)(2,1)}), bf16[32,2,128]{2,1,0:T(2,128)(2,1)S(1)}, u32[]{:S(2)}, u32[]{:S(2)}) async-start(bf16[32,2,128]{2,1,0:T(2,128)(2,1)} %reshape.373), calls=%async_computation.2 | async-start | bytes 32768 | tf_op jit(solution)/shard_map/all_to_all | solution.py:157
  211.8 8.5 %all-to-all-done.2 = bf16[32,2,128]{2,1,0:T(2,128)(2,1)S(1)} async-done(((bf16[32,2,128]{2,1,0:T(2,128)(2,1)}), bf16[32,2,128]{2,1,0:T(2,128)(2,1)S(1)}, u32[]{:S(2)}, u32[]{:S(2)}) %all-to-all-start.2) | async-done | bytes 16416 | tf_op jit(solution)/shard_map/all_to_all | solution.py:157
  220.7 24.8 %all_gather.3 = bf16[512,16,16]{1,0,2:T(8,128)(2,1)S(1)} all-gather(bf16[32,16,16]{1,0,2:T(8,128)(2,1)S(1)} %all_to_all.35), channel_id=1, replica_groups=mesh['crate'=32,'board'=16] {'board'}, dimensions={0}, use_global_device_ids=true | all-gather | bytes 278528 | tf_op jit(solution)/shard_map/all_gather | solution.py:159
  245.5 3.1 copy.54
  248.9 33.1 %scatter_fusion = bf16[512,16,16]{2,1,0:T(8,128)(2,1)S(1)} fusion(bf16[512,16,16]{2,1,0:T(8,128)(2,1)S(1)} %broadcast_in_dim.62, s32[512]{0:T(512)S(1)} %bitcast.123, bf16[512,16,16]{2,1,0:T(8,128)(2,1)} %copy.54), kind=kCustom, calls=%fused_computation.4 | custom fusion | bytes 788480 | tf_op jit(solution)/shard_map/scatter | solution.py:167
  282.0 1.9 copy.55
  284.8 195.4 %while.34 = (s32[]{:T(128)}, f32[32,32,16]{1,0,2:T(8,128)S(1)}, f32[32,32,16]{1,0,2:T(8,128)S(1)}, s32[32]{0:T(128)S(1)}, s32[256,32]{1,0:T(8,128)S(1)}, /*index...) while((s32[]{:T(128)}, f32[32,32,16]{1,0,2:T(8,128)S(1)}, ...), condition=%wide.region_5.7_spmd, body=%wide.region_4.6_spmd.sunk | while | flops 6751234 | bytes 282757 | solution.py:76
  286.7 1.3 convolution_add_fusion.2
  289.5 1.3 convolution_subtract_fusion.3
  292.9 1.3 convolution_add_fusion.2
  295.6 1.3 convolution_subtract_fusion.3
  299.0 1.3 convolution_add_fusion.2
  301.7 1.3 convolution_subtract_fusion.3
  305.1 1.3 convolution_add_fusion.2
  307.8 1.3 convolution_subtract_fusion.3
  (312 shorter events, 192.9 us)
Async XLA Ops:
  0.0 91.7 %copy-start = (s32[256,512]{1,0:T(8,128)S(1)}, s32[256,512]{1,0:T(8,128)}, u32[]{:S(2)}) copy-start(s32[256,512]{1,0:T(8,128)} %param.17) | copy-start | bytes 1572868
  5.6 15.5 %copy-start.4 = (f32[2,2048]{1,0:T(2,128)S(1)}, f32[2,2048]{1,0:T(2,128)}, u32[]{:S(2)}) copy-start(f32[2,2048]{1,0:T(2,128)} %param.14) | copy-start | bytes 49156
  5.6 15.6 %copy-start.1 = (s32[2048]{0:T(1024)S(1)}, s32[2048]{0:T(1024)}, u32[]{:S(2)}) copy-start(s32[2048]{0:T(1024)} %param.13) | copy-start | bytes 24580
  7.0 75.2 %all-to-all-start = ((bf16[32,16,1,4,128]{4,1,3,2,0:T(8,128)(2,1)}), bf16[32,16,1,4,128]{4,1,3,2,0:T(8,128)(2,1)S(1)}, u32[]{:S(2)}, u32[]{:S(2)}) async-start(bf16[32,16,1,4,128]{4,1,3,2,0:T(8,128)(2,1)} %copy.49), calls=%async_computation | async-start | bytes 1048576 | tf_op jit(solution)/shard_map/all_to_all | solution.py:112
  21.2 11.8 %copy-start.2 = (f32[2,8,2048]{2,1,0:T(8,128)S(1)}, f32[2,8,2048]{2,1,0:T(8,128)}, u32[]{:S(2)}) copy-start(f32[2,8,2048]{2,1,0:T(8,128)} %param.16) | copy-start | bytes 393220
  83.1 67.5 %all-to-all-start.1 = ((bf16[1,16,1,128,128]{4,3,2,0,1:T(8,128)(2,1)}), bf16[1,16,1,128,128]{4,3,2,0,1:T(8,128)(2,1)}, u32[]{:S(2)}, u32[]{:S(2)}) async-start(bf16[1,16,1,128,128]{4,3,2,0,1:T(8,128)(2,1)} %copy.50), calls=%async_computation.1 | async-start | bytes 1048576 | tf_op jit(solution)/shard_map/all_to_all | solution.py:111
  93.5 57.1 %copy-start.3 = (f32[2,512]{1,0:T(2,128)S(1)}, f32[2,512]{1,0:T(2,128)}, u32[]{:S(2)}) copy-start(f32[2,512]{1,0:T(2,128)} %param.15) | copy-start | bytes 12292
  202.2 18.0 %all-to-all-start.2 = ((bf16[32,2,128]{2,1,0:T(2,128)(2,1)}), bf16[32,2,128]{2,1,0:T(2,128)(2,1)S(1)}, u32[]{:S(2)}, u32[]{:S(2)}) async-start(bf16[32,2,128]{2,1,0:T(2,128)(2,1)} %reshape.373), calls=%async_computation.2 | async-start | bytes 32768 | tf_op jit(solution)/shard_map/all_to_all | solution.py:157
where the time goes:
time: 490 us; the launch traced here: 482 us
  matrix products  208 us (42%)
  local copies, waits for them, and re-layouts  180 us (37%)
  starting transfers between devices  31.8 us (6%)
  blocking collectives  24.8 us (5%)
  loops' own time  14.4 us (3%)
  other arithmetic  14.1 us (3%)
  waiting for transfers between devices  8.51 us (2%)
    dynamic_slice x1, local copies, waits for them, and re-layouts, group_power(): lax.dynamic_index_in_dim(gains_slot[1], gain_row, 0, keepdims=False)  57 us
    dot_general x32, matrix products, per_freq(): jnp.einsum('cd,cb->db', shift_im, part_re, precision=lax.Precision.HIGHEST)  42.6 us
    dot_general x32, matrix products, per_freq(): jnp.einsum('cd,cb->db', shift_im, part_im, precision=lax.Precision.HIGHEST)  42.6 us
    dot_general x32, matrix products, per_freq(): jnp.einsum('cd,cb->db', shift_re, part_re, precision=lax.Precision.HIGHEST)  42.1 us
    dot_general x32, matrix products, per_freq(): jnp.einsum('cd,cb->db', shift_re, part_im, precision=lax.Precision.HIGHEST)  42 us
    scatter x1, local copies, waits for them, and re-layouts, shards(): table = empty_table.at[whole_ids].set(portion)  33.1 us
    all_gather x1, blocking collectives, shards(): portion = lax.all_gather(regrouped, 'board', axis=0, tiled=True)  24.8 us
    dynamic_slice x64, local copies, waits for them, and re-layouts, dedisperse(): freq_re, freq_im = lax.map(per_freq, (bin_ids, spec_re, spec_im))  20 us
  transfers between devices with their start and end apart: 3, of which 1 were waited for; matrix products, arithmetic and copies ran while one was open for 25% of the time, Pallas kernels for 0%

commit v1 on v0

v1 whole, which is shorter than its diff:
```python
import functools
import math

import jax
import jax.numpy as jnp
import numpy as np
from jax import lax
from jax.experimental import pallas as pl
from jax.experimental.pallas import tpu as pltpu
from jax.sharding import PartitionSpec as P

AVG = 4
TB = 32
LOCAL_ANTENNAS = 4
SPECTRA = 128
LANES = 128
ROWS = 64
MESH = pl.DeviceIdType.MESH
F32 = jnp.float32
BF16 = jnp.bfloat16

NT = (((1,), (1,)), ((), ()))
TN = (((0,), (0,)), ((), ()))
NN = (((1,), (0,)), ((), ()))


def half_angle_coefficients():
    nodes = np.cos((np.arange(400) + 0.5) * np.pi / 400) * 0.125 + 0.125
    root = np.sqrt(nodes)
    sine = np.polynomial.chebyshev.Chebyshev.fit(
        nodes, np.sin(np.pi * root) / root, 4, domain=[0, 0.25]
    ).convert(kind=np.polynomial.Polynomial)
    cosine = np.polynomial.chebyshev.Chebyshev.fit(
        nodes, np.cos(np.pi * root), 5, domain=[0, 0.25]
    ).convert(kind=np.polynomial.Polynomial)
    return [float(x) for x in sine.coef], [float(x) for x in cosine.coef]


def filter_rows(channels, n_c, n_y):
    frame = 2 * channels
    sample = np.arange(frame)
    window = 0.5 - 0.5 * np.cos(2 * np.pi / frame * sample)
    channel = (np.arange(n_c)[None, :] * n_y + np.arange(n_y)[:, None]).reshape(-1)
    angle = 2 * np.pi / frame * (channel[:, None] * sample[None, :] % frame)
    scale = 1.0 / math.sqrt(3.0 * frame / 8.0)
    table = np.concatenate([np.cos(angle), -np.sin(angle)], axis=0) * window[None, :] * scale
    return jnp.asarray(table.astype(np.float32)).astype(BF16)


def dot(a, b, dims):
    return lax.dot_general(a, b, dims, preferred_element_type=F32)


def rotate(x, k):
    axis = x.ndim - 1
    width = x.shape[axis]
    t = lax.broadcasted_iota(jnp.int32, x.shape, axis) % TB
    near = pltpu.roll(x, width - k, axis)
    far = pltpu.roll(x, TB - k, axis)
    return jnp.where(t < TB - k, near, far)


def kernel(
    n_c,
    n_y,
    volt_ref,
    filt_ref,
    wiring_ref,
    pos_ref,
    dir_ref,
    gains_ref,
    delays_ref,
    out_ref,
    spec_ref,
    got_ref,
    turn_ref,
    col_ref,
    tab_ref,
    dirs_ref,
    wre_ref,
    wim_ref,
    give_ref,
    take_ref,
    piece_ref,
    part_ref,
    pow_ref,
    dm_ref,
    hot_ref,
    y_send,
    y_recv,
    c_send,
    c_recv,
    x_send,
    x_recv,
    p_send,
    p_recv,
    g_send,
    g_recv,
    f_send,
    own_sem,
):
    c = lax.axis_index("crate")
    board = lax.axis_index("board")
    y = board // 2
    k = board % 2
    channels = n_c * n_y
    antennas = 8 * channels
    plane = 4 * channels
    beams = 16 * n_c
    half_beams = beams // 2
    half_c = n_c // 2
    partner = (c, 2 * y + 1 - k)

    barrier = pltpu.get_barrier_semaphore()

    def greet_y(i, carry):
        peer = lax.rem(y + i, n_y)
        pl.semaphore_signal(barrier, inc=1, device_id=(c, 2 * peer + k), device_id_type=MESH)
        return carry

    def greet_c(i, carry):
        peer = lax.rem(c + i, n_c)
        pl.semaphore_signal(barrier, inc=1, device_id=(peer, board), device_id_type=MESH)
        return carry

    lax.fori_loop(1, n_y, greet_y, 0)
    lax.fori_loop(1, n_c, greet_c, 0)
    pl.semaphore_signal(barrier, inc=1, device_id=partner, device_id_type=MESH)

    for a in range(LOCAL_ANTENNAS):
        for part in range(2):
            rows = dot(filt_ref[part * channels : (part + 1) * channels, :], volt_ref[a], NT)
            spec_ref[:, a, :, part * SPECTRA : (part + 1) * SPECTRA] = rows.astype(BF16).reshape(
                n_y, n_c, SPECTRA
            )

    pl.semaphore_wait(barrier, n_y + n_c - 1)

    def y_copy(to, source, slot):
        return pltpu.make_async_remote_copy(
            src_ref=spec_ref.at[to],
            dst_ref=got_ref.at[source],
            send_sem=y_send.at[slot],
            recv_sem=y_recv.at[source],
            device_id=(c, 2 * to + k),
            device_id_type=MESH,
        )

    def y_start(i, carry):
        y_copy(lax.rem(y + i, n_y), y, i).start()
        return carry

    lax.fori_loop(1, n_y, y_start, 0)
    own_y = pltpu.make_async_copy(spec_ref.at[y], got_ref.at[y], own_sem.at[0])
    own_y.start()

    lane = lax.broadcasted_iota(jnp.int32, (plane // LANES, LANES), 1)
    even = wiring_ref[pl.ds(0, plane // LANES, stride=2), :]
    odd = wiring_ref[pl.ds(1, plane // LANES, stride=2), :]
    pick = (8 * (lane // 4) + 4 * k + lane % 4) % LANES
    ids = jnp.where(
        lane < LANES // 2,
        jnp.take_along_axis(even, pick, axis=1, mode="promise_in_bounds"),
        jnp.take_along_axis(odd, pick, axis=1, mode="promise_in_bounds"),
    )
    group = ids // LANES
    within = ids % LANES
    channel = c * n_y + y
    per_turn = 1.0 + channel.astype(F32) / channels
    norm = 1.0 / math.sqrt(antennas)

    def look_up(row_of):
        found = jnp.zeros(ids.shape, F32)
        for h in range(antennas // LANES):
            row = jnp.broadcast_to(row_of(slice(h * LANES, (h + 1) * LANES)), ids.shape)
            got = jnp.take_along_axis(row, within, axis=1, mode="promise_in_bounds")
            found = jnp.where(group == h, got, found)
        return found

    tab_ref[0] = look_up(lambda s: pos_ref[0:1, s]) * per_turn
    tab_ref[1] = look_up(lambda s: pos_ref[1:2, s]) * per_turn
    own_row = lax.broadcasted_iota(jnp.int32, (n_y, LANES), 0) == y

    def gain_row(part, s):
        return jnp.sum(jnp.where(own_row, gains_ref[part, :, s], 0.0), axis=0, keepdims=True)

    g_re = look_up(lambda s: gain_row(0, s)) * norm
    g_im = look_up(lambda s: gain_row(1, s)) * norm
    tab_ref[2] = g_re
    tab_ref[3] = g_im
    tab_ref[4] = 2.0 * g_re
    tab_ref[5] = 2.0 * g_im
    for i in range(2):
        dirs_ref[i] = jnp.broadcast_to(dir_ref[i : i + 1, :], (LANES, beams)).T

    sine, cosine = half_angle_coefficients()
    blocks = beams // ROWS

    def weights_block(i, carry):
        r = i // blocks
        first = pl.multiple_of(lax.rem(i, blocks) * ROWS, ROWS)
        columns = pl.ds(pl.multiple_of(r * LANES, LANES), LANES)
        px, py, gr, gi, gr2, gi2 = [tab_ref[n, pl.ds(r, 1), :] for n in range(6)]
        turns = dirs_ref[0, pl.ds(first, ROWS), :] * px + dirs_ref[1, pl.ds(first, ROWS), :] * py
        turn = turns - jnp.round(turns)
        square = turn * turn
        s = sine[-1]
        for coefficient in sine[-2::-1]:
            s = s * square + coefficient
        s = s * turn
        q = cosine[-1]
        for coefficient in cosine[-2::-1]:
            q = q * square + coefficient
        wre_ref[pl.ds(first, ROWS), columns] = (gr + s * (gi2 * q - gr2 * s)).astype(BF16)
        wim_ref[pl.ds(first, ROWS), columns] = (gi - s * (gi2 * s + gr2 * q)).astype(BF16)
        return carry

    steps = plane // LANES * blocks
    lax.fori_loop(0, steps // 2, weights_block, 0)

    own_y.wait()

    def y_wait(i, carry):
        source = lax.rem(y + n_y - i, n_y)
        y_copy(source, source, i).wait_recv()
        return carry

    lax.fori_loop(1, n_y, y_wait, 0)

    received = got_ref[...].reshape(n_y * LOCAL_ANTENNAS, n_c, 2 * SPECTRA)
    turn_ref[...] = jnp.swapaxes(received, 0, 1)

    def c_copy(to, source, slot):
        return pltpu.make_async_remote_copy(
            src_ref=turn_ref.at[to],
            dst_ref=col_ref.at[source],
            send_sem=c_send.at[slot],
            recv_sem=c_recv.at[source],
            device_id=(to, board),
            device_id_type=MESH,
        )

    def c_start(i, carry):
        c_copy(lax.rem(c + i, n_c), c, i).start()
        return carry

    lax.fori_loop(1, n_c, c_start, 0)
    own_c = pltpu.make_async_copy(turn_ref.at[c], col_ref.at[c], own_sem.at[1])
    own_c.start()

    lax.fori_loop(steps // 2, steps, weights_block, 0)

    offset = pl.multiple_of(board // 4 * LANES, LANES)
    values = delays_ref[:, pl.ds(offset, LANES)].astype(F32).astype(BF16)
    source = lax.broadcasted_iota(jnp.int32, (channels, channels), 0)
    place = lax.broadcasted_iota(jnp.int32, (channels, channels), 1)
    moved = (source == place % n_c * n_y + place // n_c).astype(F32).astype(BF16)
    dm_ref[...] = dot(values, moved, TN)
    mine = dm_ref[pl.ds(pl.multiple_of(board % 4 * TB, TB), TB), :]
    for d in range(TB):
        hot_ref[d * TB : (d + 1) * TB, :] = (mine == float(d)).astype(F32).astype(BF16)

    own_c.wait()

    def c_wait(i, carry):
        source = lax.rem(c + n_c - i, n_c)
        c_copy(source, source, i).wait_recv()
        return carry

    lax.fori_loop(1, n_c, c_wait, 0)

    columns = col_ref[...].reshape(plane, 2 * SPECTRA)

    def beams_of(which):
        rows = pl.ds(pl.multiple_of(which * half_beams, half_beams), half_beams)
        with_re = dot(wre_ref[rows, :], columns, NN)
        with_im = dot(wim_ref[rows, :], columns, NN)
        return (
            with_re[:, :SPECTRA] - with_im[:, SPECTRA:],
            with_re[:, SPECTRA:] + with_im[:, :SPECTRA],
        )

    give_re, give_im = beams_of(1 - k)
    give_ref[0] = give_re
    give_ref[1] = give_im
    swap = pltpu.make_async_remote_copy(
        src_ref=give_ref,
        dst_ref=take_ref,
        send_sem=x_send,
        recv_sem=x_recv,
        device_id=partner,
        device_id_type=MESH,
    )
    swap.start()
    keep_re, keep_im = beams_of(k)
    swap.wait_recv()
    beam_re = keep_re + take_ref[0]
    beam_im = keep_im + take_ref[1]
    energy = beam_re * beam_re + beam_im * beam_im

    high = energy.astype(BF16)
    low = (energy - high.astype(F32)).astype(BF16)
    from_s = lax.broadcasted_iota(jnp.int32, (SPECTRA, LANES), 0)
    to_t = lax.broadcasted_iota(jnp.int32, (SPECTRA, LANES), 1)
    mean = jnp.where(from_s // AVG == to_t % TB, 1.0 / AVG, 0.0).astype(BF16)
    power = dot(high, mean, NN) + dot(low, mean, NN)
    beam = lax.broadcasted_iota(jnp.int32, (half_beams, LANES), 0)
    slot = lax.broadcasted_iota(jnp.int32, (half_beams, LANES), 1)
    power = jnp.where(beam % 4 == slot // TB, power, 0.0).astype(BF16)
    to_row = lax.broadcasted_iota(jnp.int32, (8 * half_c, half_beams), 0)
    of_beam = lax.broadcasted_iota(jnp.int32, (8 * half_c, half_beams), 1)
    gather = (of_beam // 16 == to_row // 8) & (of_beam % 16 // 4 == to_row % 8)
    piece_ref[...] = dot(gather.astype(F32).astype(BF16), power, NN).reshape(half_c, 8, LANES)

    def p_copy(index, source, to):
        return pltpu.make_async_remote_copy(
            src_ref=piece_ref.at[index],
            dst_ref=part_ref.at[source],
            send_sem=p_send.at[index],
            recv_sem=p_recv.at[source],
            device_id=(to, board),
            device_id_type=MESH,
        )

    def p_start(i, carry):
        to = k * half_c + i

        @pl.when(to != c)
        def _():
            p_copy(i, c, to).start()

        return carry

    lax.fori_loop(0, half_c, p_start, 0)
    holds = c // half_c == k

    def g_copy(to, source, sem, device):
        return pltpu.make_async_remote_copy(
            src_ref=pow_ref.at[source],
            dst_ref=pow_ref.at[source],
            send_sem=sem.at[to],
            recv_sem=g_recv.at[source],
            device_id=device,
            device_id_type=MESH,
        )

    @pl.when(holds)
    def _():
        own_p = pltpu.make_async_copy(
            piece_ref.at[lax.rem(c, half_c)], part_ref.at[c], own_sem.at[2]
        )
        own_p.start()
        own_p.wait()

        def p_wait(i, carry):
            source = lax.rem(c + i, n_c)
            p_copy(0, source, source).wait_recv()
            return carry

        lax.fori_loop(1, n_c, p_wait, 0)
        for j in range(4):
            pow_ref[y, :, j * LANES : (j + 1) * LANES] = part_ref[:, j, :].astype(BF16)

        def g_start(i, carry):
            to = lax.rem(y + i, n_y)
            g_copy(to, y, g_send, (c, 2 * to + k)).start()
            return carry

        lax.fori_loop(1, n_y, g_start, 0)
        g_copy(y, y, f_send, partner).start()

        def g_wait(i, carry):
            source = lax.rem(y + n_y - i, n_y)
            g_copy(source, source, g_send, (c, 2 * source + k)).wait_recv()
            g_copy(source, source, f_send, partner).start()
            return carry

        lax.fori_loop(1, n_y, g_wait, 0)

    @pl.when(jnp.logical_not(holds))
    def _():
        def f_wait(i, carry):
            g_copy(i, i, f_send, partner).wait_recv()
            return carry

        lax.fori_loop(0, n_y, f_wait, 0)

    for j in range(4):
        series = pow_ref[:, :, j * LANES : (j + 1) * LANES].reshape(channels, LANES)
        total = dot(hot_ref[...], series, NN)
        step = TB // 2
        while step:
            rows = step * TB
            total = total[:rows] + rotate(total[rows:], step)
            step //= 2
        mean_of = total
        step = TB // 2
        while step:
            mean_of = mean_of + rotate(mean_of, step)
            step //= 2
        result = (total - mean_of * (1.0 / TB)) * (1.0 / math.sqrt(channels))
        for q in range(4):
            out_ref[4 * j + q] = result[:, q * TB : (q + 1) * TB]

    def y_sent(i, carry):
        y_copy(lax.rem(y + i, n_y), y, i).wait_send()
        return carry

    lax.fori_loop(1, n_y, y_sent, 0)

    def c_sent(i, carry):
        c_copy(lax.rem(c + i, n_c), c, i).wait_send()
        return carry

    lax.fori_loop(1, n_c, c_sent, 0)
    swap.wait_send()

    def p_sent(i, carry):
        to = k * half_c + i

        @pl.when(to != c)
        def _():
            p_copy(i, c, to).wait_send()

        return carry

    lax.fori_loop(0, half_c, p_sent, 0)

    @pl.when(holds)
    def _():
        def g_sent(i, carry):
            to = lax.rem(y + i, n_y)
            g_copy(to, y, g_send, (c, 2 * to + k)).wait_send()
            g_copy(to, to, f_send, partner).wait_send()
            return carry

        lax.fori_loop(1, n_y, g_sent, 0)
        g_copy(y, y, f_send, partner).wait_send()


def shards(n_c, n_y, voltages, wiring, positions, directions, gains, delays):
    channels = n_c * n_y
    frame = 2 * channels
    plane = 4 * channels
    beams = 16 * n_c
    half_beams = beams // 2
    frames = voltages.reshape(LOCAL_ANTENNAS, SPECTRA, frame)
    table = filter_rows(channels, n_c, n_y)
    ids = wiring.reshape(-1, LANES)
    dma = pltpu.SemaphoreType.DMA
    vmem = pl.BlockSpec(memory_space=pltpu.VMEM)
    return pl.pallas_call(
        functools.partial(kernel, n_c, n_y),
        out_shape=jax.ShapeDtypeStruct((16, TB, TB), F32),
        in_specs=[vmem] * 7,
        out_specs=vmem,
        scratch_shapes=[
            pltpu.VMEM((n_y, LOCAL_ANTENNAS, n_c, 2 * SPECTRA), BF16),
            pltpu.VMEM((n_y, LOCAL_ANTENNAS, n_c, 2 * SPECTRA), BF16),
            pltpu.VMEM((n_c, LOCAL_ANTENNAS * n_y, 2 * SPECTRA), BF16),
            pltpu.VMEM((n_c, LOCAL_ANTENNAS * n_y, 2 * SPECTRA), BF16),
            pltpu.VMEM((6, plane // LANES, LANES), F32),
            pltpu.VMEM((2, beams, LANES), F32),
            pltpu.VMEM((beams, plane), BF16),
            pltpu.VMEM((beams, plane), BF16),
            pltpu.VMEM((2, half_beams, SPECTRA), F32),
            pltpu.VMEM((2, half_beams, SPECTRA), F32),
            pltpu.VMEM((n_c // 2, 8, LANES), F32),
            pltpu.VMEM((n_c, 8, LANES), F32),
            pltpu.VMEM((n_y, n_c, 4 * LANES), BF16),
            pltpu.VMEM((LANES, channels), F32),
            pltpu.VMEM((TB * TB, channels), BF16),
            dma((n_y,)),
            dma((n_y,)),
            dma((n_c,)),
            dma((n_c,)),
            dma,
            dma,
            dma((n_c // 2,)),
            dma((n_c,)),
            dma((n_y,)),
            dma((n_y,)),
            dma((n_y,)),
            dma((3,)),
        ],
        compiler_params=pltpu.CompilerParams(
            collective_id=0, has_side_effects=True, vmem_limit_bytes=60 * 1024 * 1024
        ),
    )(frames, table, ids, positions, directions, gains, delays)


def solution(mesh):
    n_c = mesh.shape["crate"]
    n_y = mesh.shape["board"] // 2
    in_specs = (P(("crate", "board"), None), P(), P(), P(), P(None, "crate", None), P())
    return jax.shard_map(
        functools.partial(shards, n_c, n_y),
        mesh=mesh,
        in_specs=in_specs,
        out_specs=P("crate", "board", None),
        check_vma=False,
    )
```

time: 490 us -> 68.7 us (0.14); the launches traced: 482 us -> 68.4 us
  matrix products: 208 us -> 0 us
  local copies, waits for them, and re-layouts: 180 us -> 3.59 us
  Pallas kernels: 0 us -> 64.8 us
  starting transfers between devices: 31.8 us -> 0 us
  blocking collectives: 24.8 us -> 0 us
  loops' own time: 14.4 us -> 0 us
  other arithmetic: 14.1 us -> 0 us
  waiting for transfers between devices: 8.51 us -> 0 us
    dot_general x137 -> x0, matrix products: 208 us -> none  [the longest x32 42.6 us: per_freq(): jnp.einsum('cd,cb->db', shift_im, part_re, precision=lax.Precision.HIGHEST)]
    dynamic_slice x66 -> x0, local copies, waits for them, and re-layouts: 77.1 us -> none  [the longest x1 57 us: group_power(): lax.dynamic_index_in_dim(gains_slot[1], gain_row, 0, keepdims=False)]
    pallas_call x0 -> x1, Pallas kernels: none -> 64.8 us  [shards(): pl.pallas_call(functools.partial(kernel, n_c, n_y), out_shape=jax.ShapeDt...]
    gather x4 -> x0, local copies, waits for them, and re-layouts: 49.9 us -> none  [the longest x1 14.5 us: shards(): gains_slot = jnp.take(gains, antenna, axis=2)]
    scatter x1 -> x0, local copies, waits for them, and re-layouts: 33.1 us -> none  [shards(): table = empty_table.at[whole_ids].set(portion)]
    all_to_all x3 -> x0, starting transfers between devices: 31.8 us -> none  [the longest x1 13.7 us: shards(): lax.all_to_all(spectrum_rows, 'crate', split_axis=0, concat_axis=3, tiled...]
    all_gather x1 -> x0, blocking collectives: 24.8 us -> none  [shards(): portion = lax.all_gather(regrouped, 'board', axis=0, tiled=True)]
    another operation x2 -> x0, loops' own time: 14.4 us -> none  [the longest x1 12.1 us: group_power(): return lax.map(block_power, dir_blocks).reshape(BEAMS, BINS)]
  transfers between devices with their start and end apart: 3 -> 0, of which waited for: 1 -> 0; matrix products, arithmetic and copies ran while one was open for 25% -> 0% of each run, Pallas kernels for 0% -> 0%
where the time goes in v1:
time: 68.7 us; the launch traced here: 68.4 us
  Pallas kernels  64.8 us (94%)
  local copies, waits for them, and re-layouts  3.59 us (5%)
    pallas_call x1, Pallas kernels, shards(): pl.pallas_call(functools.partial(kernel, n_c, n_y), out_shape=jax.ShapeDt...  64.8 us
    unnamed x2, local copies, waits for them, and re-layouts  3.59 us

profile of v1, /device:TPU:1, one launch (start us, length us, event | category | flops | bytes accessed | tf_op | source)
XLA Modules:
  0.0 68.4 jit_solution(6289175615334857608)
XLA Ops:
  0.0 1.9 %copy.10 = bf16[1,4,128,512]{3,2,1,0:T(8,128)(2,1)} copy(bf16[1,4,128,512]{3,1,2,0:T(4,128)(2,1)} %bitcast.6) | data formatting | bytes 1048576
  1.9 64.8 %shard_map.73 = f32[16,32,32]{2,1,0:T(8,128)} custom-call(bf16[4,128,512]{2,1,0:T(8,128)(2,1)} %bitcast.5, bf16[512,512]{1,0:T(8,128)(2,1)} %constant.5.filt_ref, s32[16,128]{1,0:T(8,128)} %bitcast.7, f32[2,2048]{1,0:T(2,128)} %pos_ref.1, f32[2,512]{1,0:T(2,128)} %dir_ref.1, f32[2,8,2048]{2,1,0:T(8,128)} %gains_ref.1, s32[256,512]{1,0:T(8,128)} %delays_ref.1), custom_call_target="tpu_custom_call" | custom-call | tf_op jit(solution)/shard_map/pallas_call | solution.py:452
  66.8 1.7 %copy.12 = f32[16,32,32]{2,1,0:T(8,128)} copy(f32[16,32,32]{2,1,0:T(8,128)} %shard_map.73) | data formatting | bytes 131072

commit v2 on v1

v2 whole, which is shorter than its diff:
```python
import functools
import math

import jax
import jax.numpy as jnp
import numpy as np
from jax import lax
from jax.experimental import pallas as pl
from jax.experimental.pallas import tpu as pltpu
from jax.sharding import PartitionSpec as P

AVG = 4
TB = 32
LOCAL_ANTENNAS = 4
SPECTRA = 128
LANES = 128
ROWS = 64
MESH = pl.DeviceIdType.MESH
F32 = jnp.float32
BF16 = jnp.bfloat16

NT = (((1,), (1,)), ((), ()))
TN = (((0,), (0,)), ((), ()))
NN = (((1,), (0,)), ((), ()))


def half_angle_coefficients():
    nodes = np.cos((np.arange(400) + 0.5) * np.pi / 400) * 0.125 + 0.125
    root = np.sqrt(nodes)
    sine = np.polynomial.chebyshev.Chebyshev.fit(
        nodes, np.sin(np.pi * root) / root, 4, domain=[0, 0.25]
    ).convert(kind=np.polynomial.Polynomial)
    cosine = np.polynomial.chebyshev.Chebyshev.fit(
        nodes, np.cos(np.pi * root), 5, domain=[0, 0.25]
    ).convert(kind=np.polynomial.Polynomial)
    return [float(x) for x in sine.coef], [float(x) for x in cosine.coef]


def filter_rows(channels, n_c, n_y):
    frame = 2 * channels
    sample = np.arange(frame)
    window = 0.5 - 0.5 * np.cos(2 * np.pi / frame * sample)
    channel = (np.arange(n_c)[None, :] * n_y + np.arange(n_y)[:, None]).reshape(-1)
    angle = 2 * np.pi / frame * (channel[:, None] * sample[None, :] % frame)
    scale = 1.0 / math.sqrt(3.0 * frame / 8.0)
    table = np.concatenate([np.cos(angle), -np.sin(angle)], axis=0) * window[None, :] * scale
    return jnp.asarray(table.astype(np.float32)).astype(BF16)


def dot(a, b, dims):
    return lax.dot_general(a, b, dims, preferred_element_type=F32)


def rotate(x, k):
    lane = lax.broadcasted_iota(jnp.int32, x.shape, x.ndim - 1)
    return jnp.take_along_axis(
        x, lane // TB * TB + (lane + k) % TB, axis=x.ndim - 1, mode="promise_in_bounds"
    )


def kernel(
    n_c,
    n_y,
    volt_hbm,
    filt_hbm,
    wiring_hbm,
    pos_hbm,
    dir_hbm,
    gains_hbm,
    delays_hbm,
    out_ref,
    volt_ref,
    filt_ref,
    wiring_ref,
    pos_ref,
    dir_ref,
    gains_ref,
    delays_ref,
    a_spec,
    a_got,
    a_turn,
    b_spec,
    b_got,
    b_turn,
    col_ref,
    tab_ref,
    dirs_ref,
    wre_ref,
    wim_ref,
    give_ref,
    take_ref,
    piece_ref,
    pow_ref,
    dm_ref,
    hot_ref,
    in_sem,
    ay_send,
    ay_recv,
    ac_send,
    ac_recv,
    by_send,
    by_recv,
    bc_send,
    bc_recv,
    x_send,
    x_recv,
    p_send,
    p_recv,
    f_send,
    own_sem,
):
    c = lax.axis_index("crate")
    board = lax.axis_index("board")
    y = board // 2
    k = board % 2
    channels = n_c * n_y
    antennas = 8 * channels
    plane = 4 * channels
    beams = 16 * n_c
    half_beams = beams // 2
    half_c = n_c // 2
    partner = (c, 2 * y + 1 - k)

    offset = pl.multiple_of(board // 4 * LANES, LANES)
    pairs = [
        (volt_hbm, volt_ref),
        (filt_hbm, filt_ref),
        (wiring_hbm, wiring_ref),
        (pos_hbm, pos_ref),
        (dir_hbm, dir_ref),
        (gains_hbm, gains_ref),
        (delays_hbm.at[:, pl.ds(offset, LANES)], delays_ref),
    ]
    loads = [pltpu.make_async_copy(*pair, in_sem.at[i]) for i, pair in enumerate(pairs)]
    for load in loads:
        load.start()

    barrier = pltpu.get_barrier_semaphore()

    def greet_y(i, carry):
        peer = lax.rem(y + i, n_y)
        pl.semaphore_signal(barrier, inc=1, device_id=(c, 2 * peer + k), device_id_type=MESH)
        return carry

    def greet_c(i, carry):
        peer = lax.rem(c + i, n_c)
        pl.semaphore_signal(barrier, inc=1, device_id=(peer, board), device_id_type=MESH)
        return carry

    lax.fori_loop(1, n_c, greet_c, 0)
    lax.fori_loop(1, n_y, greet_y, 0)
    pl.semaphore_signal(barrier, inc=1, device_id=partner, device_id_type=MESH)

    loads[0].wait()
    loads[1].wait()
    turned = jnp.swapaxes(volt_ref[...], 0, 1)
    frame_rows = turned.shape[0] // LOCAL_ANTENNAS

    def spectra(antenna, part):
        samples = jnp.concatenate(
            [turned[LOCAL_ANTENNAS * q + antenna] for q in range(frame_rows)], axis=1
        )
        rows = dot(filt_ref[part * channels : (part + 1) * channels, :], samples, NT)
        return rows.reshape(n_y, n_c, SPECTRA)

    for part in range(2):
        lanes = slice(part * SPECTRA, (part + 1) * SPECTRA)
        both = jnp.concatenate([spectra(2, part), spectra(3, part)], axis=0)
        b_spec[:, :, lanes] = jnp.swapaxes(both, 0, 1).astype(BF16)

    def copy(src, dst, send, recv, device):
        return pltpu.make_async_remote_copy(
            src_ref=src,
            dst_ref=dst,
            send_sem=send,
            recv_sem=recv,
            device_id=device,
            device_id_type=MESH,
        )

    def over_y(src, dst, send, recv):
        def one(to, source, slot):
            device = (c, 2 * to + k)
            return copy(src(to), dst(source), send.at[slot], recv.at[source], device)

        def start(i, carry):
            one(lax.rem(y + i, n_y), y, i).start()
            return carry

        def arrive(i, carry):
            source = lax.rem(y + n_y - i, n_y)
            one(source, source, i).wait_recv()
            return carry

        def depart(i, carry):
            one(lax.rem(y + i, n_y), y, i).wait_send()
            return carry

        return [lambda f=f: lax.fori_loop(1, n_y, f, 0) for f in (start, arrive, depart)]

    def over_c(src, dst, send, recv):
        def one(to, source, slot):
            return copy(src(to), dst(source), send.at[slot], recv.at[source], (to, board))

        def start(i, carry):
            one(lax.rem(c + i, n_c), c, i).start()
            return carry

        def arrive(i, carry):
            source = lax.rem(c + n_c - i, n_c)
            one(source, source, i).wait_recv()
            return carry

        def depart(i, carry):
            one(lax.rem(c + i, n_c), c, i).wait_send()
            return carry

        return [lambda f=f: lax.fori_loop(1, n_c, f, 0) for f in (start, arrive, depart)]

    def a_rows(source):
        return col_ref.at[pl.ds(pl.multiple_of(source * 2 * n_y, 2 * n_y), 2 * n_y)]

    def b_rows(source):
        first = pl.multiple_of(plane // 2 + source * 2 * n_c, 2 * n_c)
        return col_ref.at[pl.ds(first, 2 * n_c)]

    a_one = over_y(lambda i: a_spec.at[i], lambda i: a_got.at[i], ay_send, ay_recv)
    a_two = over_c(lambda i: a_turn.at[i], a_rows, ac_send, ac_recv)
    b_one = over_c(lambda i: b_spec.at[i], lambda i: b_got.at[i], bc_send, bc_recv)
    b_two = over_y(lambda i: b_turn.at[i], b_rows, by_send, by_recv)

    pl.semaphore_wait(barrier, n_y + n_c - 1)
    b_one[0]()
    own_b = pltpu.make_async_copy(b_spec.at[c], b_got.at[c], own_sem.at[0])
    own_b.start()
    for antenna in range(2):
        for part in range(2):
            lanes = slice(part * SPECTRA, (part + 1) * SPECTRA)
            a_spec[:, antenna, :, lanes] = spectra(antenna, part).astype(BF16)
    a_one[0]()
    own_a = pltpu.make_async_copy(a_spec.at[y], a_got.at[y], own_sem.at[1])
    own_a.start()

    for load in loads[2:]:
        load.wait()
    shape = (plane // LANES, LANES)
    place = lax.broadcasted_iota(jnp.int32, shape, 0) * LANES
    place = place + lax.broadcasted_iota(jnp.int32, shape, 1)
    in_b = place - plane // 2
    of_a = (place // (2 * n_y) * 2 * n_y + place % (2 * n_y) // 2 * 2 + k) * 4 + place % 2
    of_b = (in_b % n_c * 2 * n_y + in_b // (2 * n_c) * 2 + k) * 4 + 2 + in_b // n_c % 2
    row_id = jnp.where(place < plane // 2, of_a, of_b)

    def look_up(index, row_of, dtype):
        group = index // LANES
        within = index % LANES
        found = jnp.zeros(shape, dtype)
        for h in range(antennas // LANES):
            row = jnp.broadcast_to(row_of(h), shape)
            got = jnp.take_along_axis(row, within, axis=1, mode="promise_in_bounds")
            found = jnp.where(group == h, got, found)
        return found

    def part_of(h):
        return slice(h * LANES, (h + 1) * LANES)

    ids = look_up(row_id, lambda h: wiring_ref[h : h + 1, :], jnp.int32)
    channel = c * n_y + y
    per_turn = 1.0 + channel.astype(F32) / channels
    norm = 1.0 / math.sqrt(antennas)
    own_row = lax.broadcasted_iota(jnp.int32, (n_y, LANES), 0) == y

    def gain_row(part, h):
        rows = gains_ref[part, :, part_of(h)]
        return jnp.sum(jnp.where(own_row, rows, 0.0), axis=0, keepdims=True)

    tab_ref[0] = look_up(ids, lambda h: pos_ref[0:1, part_of(h)], F32) * per_turn
    tab_ref[1] = look_up(ids, lambda h: pos_ref[1:2, part_of(h)], F32) * per_turn
    g_re = look_up(ids, lambda h: gain_row(0, h), F32) * norm
    g_im = look_up(ids, lambda h: gain_row(1, h), F32) * norm
    tab_ref[2] = g_re
    tab_ref[3] = g_im
    tab_ref[4] = 2.0 * g_re
    tab_ref[5] = 2.0 * g_im
    for i in range(2):
        dirs_ref[i] = jnp.broadcast_to(dir_ref[i : i + 1, :], (LANES, beams)).T

    sine, cosine = half_angle_coefficients()
    blocks = beams // ROWS

    def weights_block(i, carry):
        r = i // blocks
        first = pl.multiple_of(lax.rem(i, blocks) * ROWS, ROWS)
        columns = pl.ds(pl.multiple_of(r * LANES, LANES), LANES)
        px, py, gr, gi, gr2, gi2 = [tab_ref[n, pl.ds(r, 1), :] for n in range(6)]
        turns = dirs_ref[0, pl.ds(first, ROWS), :] * px + dirs_ref[1, pl.ds(first, ROWS), :] * py
        turn = turns - jnp.round(turns)
        square = turn * turn
        s = sine[-1]
        for coefficient in sine[-2::-1]:
            s = s * square + coefficient
        s = s * turn
        q = cosine[-1]
        for coefficient in cosine[-2::-1]:
            q = q * square + coefficient
        wre_ref[pl.ds(first, ROWS), columns] = (gr + s * (gi2 * q - gr2 * s)).astype(BF16)
        wim_ref[pl.ds(first, ROWS), columns] = (gi - s * (gi2 * s + gr2 * q)).astype(BF16)
        return carry

    steps = plane // LANES * blocks
    lax.fori_loop(0, steps // 2, weights_block, 0)

    own_a.wait()
    a_one[1]()
    received = a_got[...].reshape(2 * n_y, n_c, 2 * SPECTRA)
    a_turn[...] = jnp.swapaxes(received, 0, 1)
    a_two[0]()
    own_a = pltpu.make_async_copy(a_turn.at[c], a_rows(c), own_sem.at[2])
    own_a.start()

    own_b.wait()
    b_one[1]()
    received = jnp.swapaxes(b_got[...], 0, 1)
    for antenna in range(2):
        b_turn[:, antenna * n_c : (antenna + 1) * n_c, :] = received[
            antenna * n_y : (antenna + 1) * n_y
        ]
    b_two[0]()
    own_b = pltpu.make_async_copy(b_turn.at[y], b_rows(y), own_sem.at[3])
    own_b.start()

    lax.fori_loop(steps // 2, steps, weights_block, 0)

    values = delays_ref[...].astype(F32).astype(BF16)
    source = lax.broadcasted_iota(jnp.int32, (channels, channels), 0)
    position = lax.broadcasted_iota(jnp.int32, (channels, channels), 1)
    tiles = channels // 4
    piece = position % tiles * 4 + position // tiles
    moved = (source == piece % n_c * n_y + piece // n_c).astype(F32).astype(BF16)
    dm_ref[...] = dot(values, moved, TN)
    mine = dm_ref[pl.ds(pl.multiple_of(board % 4 * TB, TB), TB), :]
    for d in range(TB):
        hot_ref[d * TB : (d + 1) * TB, :] = (mine == float(d)).astype(F32).astype(BF16)

    own_a.wait()
    own_b.wait()
    a_two[1]()
    b_two[1]()

    def beams_of(which):
        rows = pl.ds(pl.multiple_of(which * half_beams, half_beams), half_beams)
        with_re = dot(wre_ref[rows, :], col_ref[...], NN)
        with_im = dot(wim_ref[rows, :], col_ref[...], NN)
        return (
            with_re[:, :SPECTRA] - with_im[:, SPECTRA:],
            with_re[:, SPECTRA:] + with_im[:, :SPECTRA],
        )

    give_re, give_im = beams_of(1 - k)
    give_ref[0] = give_re
    give_ref[1] = give_im
    swap = copy(give_ref, take_ref, x_send, x_recv, partner)
    swap.start()
    keep_re, keep_im = beams_of(k)
    swap.wait_recv()
    beam_re = keep_re + take_ref[0]
    beam_im = keep_im + take_ref[1]
    energy = beam_re * beam_re + beam_im * beam_im

    high = energy.astype(BF16)
    low = (energy - high.astype(F32)).astype(BF16)
    from_s = lax.broadcasted_iota(jnp.int32, (SPECTRA, LANES), 0)
    to_t = lax.broadcasted_iota(jnp.int32, (SPECTRA, LANES), 1)
    mean = jnp.where(from_s // AVG == to_t % TB, 1.0 / AVG, 0.0).astype(BF16)
    power = dot(high, mean, NN) + dot(low, mean, NN)
    beam = lax.broadcasted_iota(jnp.int32, (half_beams, LANES), 0)
    slot = lax.broadcasted_iota(jnp.int32, (half_beams, LANES), 1)
    power = jnp.where(beam % 4 == slot // TB, power, 0.0).astype(BF16)
    to_row = lax.broadcasted_iota(jnp.int32, (half_beams // 4, half_beams), 0)
    of_beam = lax.broadcasted_iota(jnp.int32, (half_beams // 4, half_beams), 1)
    gather = (of_beam // 4 == to_row).astype(F32).astype(BF16)
    piece_ref[...] = dot(gather, power, NN).reshape(half_c, 4, LANES).astype(BF16)

    holds = c // half_c == k
    count = half_c * n_y
    mine_at = y * n_c + c

    def p_copy(i):
        return copy(
            piece_ref.at[i // n_y],
            pow_ref.at[mine_at],
            p_send,
            p_recv.at[y],
            (k * half_c + i // n_y, 2 * lax.rem(i, n_y) + k),
        )

    def p_start(i, carry):
        away = (k * half_c + i // n_y != c) | (lax.rem(i, n_y) != y)

        @pl.when(away)
        def _():
            p_copy(i).start()

        return carry

    lax.fori_loop(0, count, p_start, 0)

    def group(source, size):
        return pow_ref.at[pl.ds(pl.multiple_of(source * n_c, n_c), size)]

    def forward(source):
        rows = group(source, n_c)
        return copy(rows, rows, f_send.at[source], p_recv.at[source], partner)

    def group_wait(source, size):
        rows = group(source, size)
        copy(rows, rows, p_send, p_recv.at[source], partner).wait_recv()

    @pl.when(holds)
    def _():
        own_p = pltpu.make_async_copy(
            piece_ref.at[lax.rem(c, half_c)], pow_ref.at[mine_at], own_sem.at[4]
        )
        own_p.start()
        own_p.wait()
        group_wait(y, n_c - 1)
        forward(y).start()

        def g_wait(i, carry):
            source = lax.rem(y + i, n_y)
            group_wait(source, n_c)
            forward(source).start()
            return carry

        lax.fori_loop(1, n_y, g_wait, 0)

    @pl.when(jnp.logical_not(holds))
    def _():
        def f_wait(i, carry):
            forward(i).wait_recv()
            return carry

        lax.fori_loop(0, n_y, f_wait, 0)

    series = jnp.swapaxes(pow_ref[...].reshape(tiles, 16, LANES), 0, 1)
    for pair in range(2):
        both = [
            jnp.concatenate([series[4 * r + 2 * pair + j] for r in range(4)], axis=0)
            for j in range(2)
        ]
        sums = dot(hot_ref[...], jnp.concatenate(both, axis=1), NN)
        for j in range(2):
            total = sums[:, j * LANES : (j + 1) * LANES]
            step = TB // 2
            while step:
                rows = step * TB
                total = total[:rows] + rotate(total[rows:], step)
                step //= 2
            mean_of = total
            step = TB // 2
            while step:
                mean_of = mean_of + rotate(mean_of, step)
                step //= 2
            result = (total - mean_of * (1.0 / TB)) * (1.0 / math.sqrt(channels))
            for q in range(4):
                out_ref[4 * (2 * pair + j) + q] = result[:, q * TB : (q + 1) * TB]

    for exchange in (b_one, a_one, a_two, b_two):
        exchange[2]()
    swap.wait_send()

    @pl.when(holds)
    def _():
        rows = pow_ref.at[pl.ds(0, count - 1)]
        copy(rows, rows, p_send, p_recv.at[0], partner).wait_send()

        def f_sent(i, carry):
            forward(i).wait_send()
            return carry

        lax.fori_loop(0, n_y, f_sent, 0)

    @pl.when(jnp.logical_not(holds))
    def _():
        rows = pow_ref.at[pl.ds(0, count)]
        copy(rows, rows, p_send, p_recv.at[0], partner).wait_send()


def shards(n_c, n_y, voltages, wiring, positions, directions, gains, delays):
    channels = n_c * n_y
    frame = 2 * channels
    plane = 4 * channels
    beams = 16 * n_c
    half_beams = beams // 2
    samples = voltages.reshape(LOCAL_ANTENNAS, SPECTRA * frame // LANES, LANES).transpose(1, 0, 2)
    samples = samples.reshape(SPECTRA, frame // LANES * LOCAL_ANTENNAS, LANES)
    table = filter_rows(channels, n_c, n_y)
    ids = wiring.reshape(-1, LANES)
    operands = (samples, table, ids, positions, directions, gains, delays)
    loaded = [pltpu.VMEM(x.shape, x.dtype) for x in operands[:-1]]
    loaded.append(pltpu.VMEM((channels, LANES), delays.dtype))
    dma = pltpu.SemaphoreType.DMA
    by_y = pltpu.VMEM((n_y, 2, n_c, 2 * SPECTRA), BF16)
    by_c = pltpu.VMEM((n_c, 2 * n_y, 2 * SPECTRA), BF16)
    return pl.pallas_call(
        functools.partial(kernel, n_c, n_y),
        out_shape=jax.ShapeDtypeStruct((16, TB, TB), F32),
        in_specs=[pl.BlockSpec(memory_space=pl.ANY)] * len(operands),
        out_specs=pl.BlockSpec(memory_space=pltpu.VMEM),
        scratch_shapes=[
            *loaded,
            by_y,
            by_y,
            by_c,
            by_c,
            by_c,
            pltpu.VMEM((n_y, 2 * n_c, 2 * SPECTRA), BF16),
            pltpu.VMEM((plane, 2 * SPECTRA), BF16),
            pltpu.VMEM((6, plane // LANES, LANES), F32),
            pltpu.VMEM((2, beams, LANES), F32),
            pltpu.VMEM((beams, plane), BF16),
            pltpu.VMEM((beams, plane), BF16),
            pltpu.VMEM((2, half_beams, SPECTRA), F32),
            pltpu.VMEM((2, half_beams, SPECTRA), F32),
            pltpu.VMEM((n_c // 2, 4, LANES), BF16),
            pltpu.VMEM((channels, 4, LANES), BF16),
            pltpu.VMEM((LANES, channels), F32),
            pltpu.VMEM((TB * TB, channels), BF16),
            dma((len(operands),)),
            dma((n_y,)),
            dma((n_y,)),
            dma((n_c,)),
            dma((n_c,)),
            dma((n_y,)),
            dma((n_y,)),
            dma((n_c,)),
            dma((n_c,)),
            dma,
            dma,
            dma,
            dma((n_y,)),
            dma((n_y,)),
            dma((5,)),
        ],
        compiler_params=pltpu.CompilerParams(
            collective_id=0, has_side_effects=True, vmem_limit_bytes=60 * 1024 * 1024
        ),
    )(*operands)


def solution(mesh):
    n_c = mesh.shape["crate"]
    n_y = mesh.shape["board"] // 2
    in_specs = (P(("crate", "board"), None), P(), P(), P(), P(None, "crate", None), P())
    return jax.shard_map(
        functools.partial(shards, n_c, n_y),
        mesh=mesh,
        in_specs=in_specs,
        out_specs=P("crate", "board", None),
        check_vma=False,
    )
```

time: 68.7 us -> 51.7 us (0.75)
  Pallas kernels: 64.8 us -> 49.8 us
  local copies, waits for them, and re-layouts: 3.59 us -> 1.67 us
    pallas_call x1, Pallas kernels: 64.8 us -> 49.8 us  [shards(): pl.pallas_call(functools.partial(kernel, n_c, n_y), out_shape=jax.ShapeDt...]
    unnamed x2 -> x1, local copies, waits for them, and re-layouts: 3.59 us -> 1.67 us
where the time goes in v2:
time: 51.7 us; the launch traced here: 51.5 us
  Pallas kernels  49.8 us (96%)
  local copies, waits for them, and re-layouts  1.67 us (3%)
    pallas_call x1, Pallas kernels, shards(): pl.pallas_call(functools.partial(kernel, n_c, n_y), out_shape=jax.ShapeDt...  49.8 us
    unnamed x1, local copies, waits for them, and re-layouts  1.67 us

profile of v2, /device:TPU:1, one launch (start us, length us, event | category | flops | bytes accessed | tf_op | source)
XLA Modules:
  0.0 51.5 jit_solution(8412510173151684784)
XLA Ops:
  0.0 49.8 %shard_map.73 = f32[16,32,32]{2,1,0:T(8,128)} custom-call(bf16[128,16,128]{2,1,0:T(8,128)(2,1)} %bitcast.6, bf16[512,512]{1,0:T(8,128)(2,1)} %constant.5.filt_hbm, s32[16,128]{1,0:T(8,128)} %bitcast.7, f32[2,2048]{1,0:T(2,128)} %pos_hbm.1, f32[2,512]{1,0:T(2,128)} %dir_hbm.1, f32[2,8,2048]{2,1,0:T(8,128)} %gains_hbm.1, s32[256,512]{1,0:T(8,128)} %delays_hbm.1), custom_call_target="tpu_custom_call" | custom-call | tf_op jit(solution)/shard_map/pallas_call | solution.py:505
  49.9 1.7 %copy.10 = f32[16,32,32]{2,1,0:T(8,128)} copy(f32[16,32,32]{2,1,0:T(8,128)} %shard_map.73) | data formatting | bytes 131072

commit v3 on v2

--- a/solution.py
+++ b/solution.py
@@ -47,6 +47,10 @@
     return jnp.asarray(table.astype(np.float32)).astype(BF16)
 
 
+def far_first(size):
+    return sorted(range(size), key=lambda d: -min(d, size - d))
+
+
 def dot(a, b, dims):
     return lax.dot_general(a, b, dims, preferred_element_type=F32)
 
@@ -68,7 +72,7 @@
     dir_hbm,
     gains_hbm,
     delays_hbm,
-    out_ref,
+    out_hbm,
     volt_ref,
     filt_ref,
     wiring_ref,
@@ -79,10 +83,11 @@
     a_spec,
     a_got,
     a_turn,
+    a_col,
     b_spec,
     b_got,
     b_turn,
-    col_ref,
+    b_col,
     tab_ref,
     dirs_ref,
     wre_ref,
@@ -93,21 +98,19 @@
     pow_ref,
     dm_ref,
     hot_ref,
+    made_ref,
     in_sem,
-    ay_send,
-    ay_recv,
-    ac_send,
-    ac_recv,
-    by_send,
-    by_recv,
-    bc_send,
-    bc_recv,
+    a_send,
+    a_recv,
+    b_send,
+    b_recv,
     x_send,
     x_recv,
     p_send,
     p_recv,
     f_send,
     own_sem,
+    out_sem,
 ):
     c = lax.axis_index("crate")
     board = lax.axis_index("board")
@@ -120,6 +123,16 @@
     half_beams = beams // 2
     half_c = n_c // 2
     partner = (c, 2 * y + 1 - k)
+    n_x = min(8, n_c)
+    n_z = n_c // n_x
+    x = c % n_x
+    z = c // n_x
+    mine_at = y * n_c + c
+
+    steps_c = [(dz, dx) for dz in range(n_z) for dx in range(n_x)]
+    steps_c.sort(key=lambda s: -min(s[0], n_z - s[0]) - min(s[1], n_x - s[1]))
+    crates = [(z + dz) % n_z * n_x + (x + dx) % n_x for dz, dx in steps_c[:-1]]
+    places = [(y + dy) % n_y for dy in far_first(n_y)[:-1]]
 
     offset = pl.multiple_of(board // 4 * LANES, LANES)
     pairs = [
@@ -136,37 +149,24 @@
         load.start()
 
     barrier = pltpu.get_barrier_semaphore()
-
-    def greet_y(i, carry):
-        peer = lax.rem(y + i, n_y)
-        pl.semaphore_signal(barrier, inc=1, device_id=(c, 2 * peer + k), device_id_type=MESH)
-        return carry
-
-    def greet_c(i, carry):
-        peer = lax.rem(c + i, n_c)
-        pl.semaphore_signal(barrier, inc=1, device_id=(peer, board), device_id_type=MESH)
-        return carry
-
-    lax.fori_loop(1, n_c, greet_c, 0)
-    lax.fori_loop(1, n_y, greet_y, 0)
-    pl.semaphore_signal(barrier, inc=1, device_id=partner, device_id_type=MESH)
+    for device in [(i, board) for i in crates] + [(c, 2 * i + k) for i in places] + [partner]:
+        pl.semaphore_signal(barrier, inc=1, device_id=device, device_id_type=MESH)
 
     loads[0].wait()
     loads[1].wait()
     turned = jnp.swapaxes(volt_ref[...], 0, 1)
     frame_rows = turned.shape[0] // LOCAL_ANTENNAS
-
-    def spectra(antenna, part):
+    for antenna in range(LOCAL_ANTENNAS):
         samples = jnp.concatenate(
             [turned[LOCAL_ANTENNAS * q + antenna] for q in range(frame_rows)], axis=1
         )
-        rows = dot(filt_ref[part * channels : (part + 1) * channels, :], samples, NT)
-        return rows.reshape(n_y, n_c, SPECTRA)
-
-    for part in range(2):
-        lanes = slice(part * SPECTRA, (part + 1) * SPECTRA)
-        both = jnp.concatenate([spectra(2, part), spectra(3, part)], axis=0)
-        b_spec[:, :, lanes] = jnp.swapaxes(both, 0, 1).astype(BF16)
+        rows = dot(filt_ref[...], samples, NT).reshape(2, n_y, n_c, SPECTRA)
+        for part in range(2):
+            lanes = slice(part * SPECTRA, (part + 1) * SPECTRA)
+            if antenna < 2:
+                a_spec[antenna, :, :, lanes] = rows[part].astype(BF16)
+            else:
+                b_spec[antenna - 2, :, :, lanes] = jnp.swapaxes(rows[part], 0, 1).astype(BF16)
 
     def copy(src, dst, send, recv, device):
         return pltpu.make_async_remote_copy(
@@ -178,78 +178,51 @@
             device_id_type=MESH,
         )
 
-    def over_y(src, dst, send, recv):
-        def one(to, source, slot):
-            device = (c, 2 * to + k)
-            return copy(src(to), dst(source), send.at[slot], recv.at[source], device)
-
-        def start(i, carry):
-            one(lax.rem(y + i, n_y), y, i).start()
-            return carry
-
-        def arrive(i, carry):
-            source = lax.rem(y + n_y - i, n_y)
-            one(source, source, i).wait_recv()
-            return carry
-
-        def depart(i, carry):
-            one(lax.rem(y + i, n_y), y, i).wait_send()
-            return carry
-
-        return [lambda f=f: lax.fori_loop(1, n_y, f, 0) for f in (start, arrive, depart)]
-
-    def over_c(src, dst, send, recv):
-        def one(to, source, slot):
-            return copy(src(to), dst(source), send.at[slot], recv.at[source], (to, board))
-
-        def start(i, carry):
-            one(lax.rem(c + i, n_c), c, i).start()
-            return carry
-
-        def arrive(i, carry):
-            source = lax.rem(c + n_c - i, n_c)
-            one(source, source, i).wait_recv()
-            return carry
-
-        def depart(i, carry):
-            one(lax.rem(c + i, n_c), c, i).wait_send()
-            return carry
-
-        return [lambda f=f: lax.fori_loop(1, n_c, f, 0) for f in (start, arrive, depart)]
-
-    def a_rows(source):
-        return col_ref.at[pl.ds(pl.multiple_of(source * 2 * n_y, 2 * n_y), 2 * n_y)]
-
-    def b_rows(source):
-        first = pl.multiple_of(plane // 2 + source * 2 * n_c, 2 * n_c)
-        return col_ref.at[pl.ds(first, 2 * n_c)]
-
-    a_one = over_y(lambda i: a_spec.at[i], lambda i: a_got.at[i], ay_send, ay_recv)
-    a_two = over_c(lambda i: a_turn.at[i], a_rows, ac_send, ac_recv)
-    b_one = over_c(lambda i: b_spec.at[i], lambda i: b_got.at[i], bc_send, bc_recv)
-    b_two = over_y(lambda i: b_turn.at[i], b_rows, by_send, by_recv)
+    class Exchange:
+        def __init__(self, src, dst, send, recv, own_sem, along_y):
+            self.refs = (src, dst)
+            self.sems = (send, recv)
+            self.here, self.others = (y, places) if along_y else (c, crates)
+            self.device = (lambda i: (c, 2 * i + k)) if along_y else (lambda i: (i, board))
+            own = (src.at[self.here], dst.at[self.here], own_sem)
+            self.own = pltpu.make_async_copy(*own)
+            count = pl.ds(0, len(self.others))
+            self.all = copy(src.at[count], dst.at[count], send, recv, partner)
+
+        def start(self):
+            src, dst = self.refs
+            for i in self.others:
+                copy(src.at[i], dst.at[self.here], *self.sems, self.device(i)).start()
+            self.own.start()
+
+        def arrive(self):
+            self.own.wait()
+            self.all.wait_recv()
+
+    a_one, a_two, b_one, b_two = [], [], [], []
+    for h in range(2):
+        a_sems = [(a_send.at[s], a_recv.at[s], own_sem.at[s]) for s in (h, 2 + h)]
+        b_sems = [(b_send.at[s], b_recv.at[s], own_sem.at[4 + s]) for s in (h, 2 + h)]
+        a_one.append(Exchange(a_spec.at[h], a_got.at[h], *a_sems[0], True))
+        a_two.append(Exchange(a_turn.at[h], a_col.at[h], *a_sems[1], False))
+        b_one.append(Exchange(b_spec.at[h], b_got.at[h], *b_sems[0], False))
+        b_two.append(Exchange(b_turn.at[h], b_col.at[h], *b_sems[1], True))
 
     pl.semaphore_wait(barrier, n_y + n_c - 1)
-    b_one[0]()
-    own_b = pltpu.make_async_copy(b_spec.at[c], b_got.at[c], own_sem.at[0])
-    own_b.start()
-    for antenna in range(2):
-        for part in range(2):
-            lanes = slice(part * SPECTRA, (part + 1) * SPECTRA)
-            a_spec[:, antenna, :, lanes] = spectra(antenna, part).astype(BF16)
-    a_one[0]()
-    own_a = pltpu.make_async_copy(a_spec.at[y], a_got.at[y], own_sem.at[1])
-    own_a.start()
+    for h in range(2):
+        a_one[h].start()
+        b_one[h].start()
 
     for load in loads[2:]:
         load.wait()
     shape = (plane // LANES, LANES)
     place = lax.broadcasted_iota(jnp.int32, shape, 0) * LANES
     place = place + lax.broadcasted_iota(jnp.int32, shape, 1)
-    in_b = place - plane // 2
-    of_a = (place // (2 * n_y) * 2 * n_y + place % (2 * n_y) // 2 * 2 + k) * 4 + place % 2
-    of_b = (in_b % n_c * 2 * n_y + in_b // (2 * n_c) * 2 + k) * 4 + 2 + in_b // n_c % 2
-    row_id = jnp.where(place < plane // 2, of_a, of_b)
+    antenna = place // channels
+    device = place % channels
+    of_a = device // n_y * 2 * n_y + device % n_y * 2 + k
+    of_b = device % n_c * 2 * n_y + device // n_c * 2 + k
+    row_id = jnp.where(antenna < 2, of_a, of_b) * 4 + antenna
 
     def look_up(index, row_of, dtype):
         group = index // LANES
@@ -309,26 +282,13 @@
 
     steps = plane // LANES * blocks
     lax.fori_loop(0, steps // 2, weights_block, 0)
-
-    own_a.wait()
-    a_one[1]()
-    received = a_got[...].reshape(2 * n_y, n_c, 2 * SPECTRA)
-    a_turn[...] = jnp.swapaxes(received, 0, 1)
-    a_two[0]()
-    own_a = pltpu.make_async_copy(a_turn.at[c], a_rows(c), own_sem.at[2])
-    own_a.start()
-
-    own_b.wait()
-    b_one[1]()
-    received = jnp.swapaxes(b_got[...], 0, 1)
-    for antenna in range(2):
-        b_turn[:, antenna * n_c : (antenna + 1) * n_c, :] = received[
-            antenna * n_y : (antenna + 1) * n_y
-        ]
-    b_two[0]()
-    own_b = pltpu.make_async_copy(b_turn.at[y], b_rows(y), own_sem.at[3])
-    own_b.start()
-
+    for h in range(2):
+        a_one[h].arrive()
+        a_turn[h] = jnp.swapaxes(a_got[h], 0, 1)
+        a_two[h].start()
+        b_one[h].arrive()
+        b_turn[h] = jnp.swapaxes(b_got[h], 0, 1)
+        b_two[h].start()
     lax.fori_loop(steps // 2, steps, weights_block, 0)
 
     values = delays_ref[...].astype(F32).astype(BF16)
@@ -342,15 +302,17 @@
     for d in range(TB):
         hot_ref[d * TB : (d + 1) * TB, :] = (mine == float(d)).astype(F32).astype(BF16)
 
-    own_a.wait()
-    own_b.wait()
-    a_two[1]()
-    b_two[1]()
+    for h in range(2):
+        a_two[h].arrive()
+        b_two[h].arrive()
+
+    rows = (2 * channels, 2 * SPECTRA)
+    columns = jnp.concatenate([a_col[...].reshape(rows), b_col[...].reshape(rows)], axis=0)
 
     def beams_of(which):
         rows = pl.ds(pl.multiple_of(which * half_beams, half_beams), half_beams)
-        with_re = dot(wre_ref[rows, :], col_ref[...], NN)
-        with_im = dot(wim_ref[rows, :], col_ref[...], NN)
+        with_re = dot(wre_ref[rows, :], columns, NN)
+        with_im = dot(wim_ref[rows, :], columns, NN)
         return (
             with_re[:, :SPECTRA] - with_im[:, SPECTRA:],
             with_re[:, SPECTRA:] + with_im[:, :SPECTRA],
@@ -383,27 +345,25 @@
 
     holds = c // half_c == k
     count = half_c * n_y
-    mine_at = y * n_c + c
-
-    def p_copy(i):
+
+    def p_copy(index, to_y):
         return copy(
-            piece_ref.at[i // n_y],
+            piece_ref.at[index],
             pow_ref.at[mine_at],
             p_send,
             p_recv.at[y],
-            (k * half_c + i // n_y, 2 * lax.rem(i, n_y) + k),
+            (k * half_c + index, 2 * to_y + k),
         )
 
-    def p_start(i, carry):
-        away = (k * half_c + i // n_y != c) | (lax.rem(i, n_y) != y)
-
-        @pl.when(away)
+    indices = [h * n_x + (x + dx) % n_x for dx in far_first(n_x) for h in range(half_c // n_x)]
+    for to_y in places:
+        for index in indices:
+            p_copy(index, to_y).start()
+    for index in indices:
+
+        @pl.when(k * half_c + index != c)
         def _():
-            p_copy(i).start()
-
-        return carry
-
-    lax.fori_loop(0, count, p_start, 0)
+            p_copy(index, y).start()
 
     def group(source, size):
         return pow_ref.at[pl.ds(pl.multiple_of(source * n_c, n_c), size)]
@@ -419,7 +379,7 @@
     @pl.when(holds)
     def _():
         own_p = pltpu.make_async_copy(
-            piece_ref.at[lax.rem(c, half_c)], pow_ref.at[mine_at], own_sem.at[4]
+            piece_ref.at[lax.rem(c, half_c)], pow_ref.at[mine_at], own_sem.at[8]
         )
         own_p.start()
         own_p.wait()
@@ -443,6 +403,11 @@
         lax.fori_loop(0, n_y, f_wait, 0)
 
     series = jnp.swapaxes(pow_ref[...].reshape(tiles, 16, LANES), 0, 1)
+
+    def put(first):
+        rows = pl.ds(first, 4)
+        return pltpu.make_async_copy(made_ref.at[rows], out_hbm.at[rows], out_sem.at[first // 4])
+
     for pair in range(2):
         both = [
             jnp.concatenate([series[4 * r + 2 * pair + j] for r in range(4)], axis=0)
@@ -462,11 +427,13 @@
                 mean_of = mean_of + rotate(mean_of, step)
                 step //= 2
             result = (total - mean_of * (1.0 / TB)) * (1.0 / math.sqrt(channels))
+            first = 4 * (2 * pair + j)
             for q in range(4):
-                out_ref[4 * (2 * pair + j) + q] = result[:, q * TB : (q + 1) * TB]
-
-    for exchange in (b_one, a_one, a_two, b_two):
-        exchange[2]()
+                made_ref[first + q] = result[:, q * TB : (q + 1) * TB]
+            put(first).start()
+
+    for one in a_one + a_two + b_one + b_two:
+        one.all.wait_send()
     swap.wait_send()
 
     @pl.when(holds)
@@ -484,6 +451,9 @@
     def _():
         rows = pow_ref.at[pl.ds(0, count)]
         copy(rows, rows, p_send, p_recv.at[0], partner).wait_send()
+
+    for first in range(0, 16, 4):
+        put(first).wait()
 
 
 def shards(n_c, n_y, voltages, wiring, positions, directions, gains, delays):
@@ -500,22 +470,17 @@
     loaded = [pltpu.VMEM(x.shape, x.dtype) for x in operands[:-1]]
     loaded.append(pltpu.VMEM((channels, LANES), delays.dtype))
     dma = pltpu.SemaphoreType.DMA
-    by_y = pltpu.VMEM((n_y, 2, n_c, 2 * SPECTRA), BF16)
-    by_c = pltpu.VMEM((n_c, 2 * n_y, 2 * SPECTRA), BF16)
+    by_y = pltpu.VMEM((2, n_y, n_c, 2 * SPECTRA), BF16)
+    by_c = pltpu.VMEM((2, n_c, n_y, 2 * SPECTRA), BF16)
     return pl.pallas_call(
         functools.partial(kernel, n_c, n_y),
         out_shape=jax.ShapeDtypeStruct((16, TB, TB), F32),
         in_specs=[pl.BlockSpec(memory_space=pl.ANY)] * len(operands),
-        out_specs=pl.BlockSpec(memory_space=pltpu.VMEM),
+        out_specs=pl.BlockSpec(memory_space=pl.ANY),
         scratch_shapes=[
             *loaded,
-            by_y,
-            by_y,
-            by_c,
-            by_c,
-            by_c,
-            pltpu.VMEM((n_y, 2 * n_c, 2 * SPECTRA), BF16),
-            pltpu.VMEM((plane, 2 * SPECTRA), BF16),
+            *[by_y, by_y, by_c, by_c],
+            *[by_c, by_c, by_y, by_y],
             pltpu.VMEM((6, plane // LANES, LANES), F32),
             pltpu.VMEM((2, beams, LANES), F32),
             pltpu.VMEM((beams, plane), BF16),
@@ -526,21 +491,16 @@
             pltpu.VMEM((channels, 4, LANES), BF16),
             pltpu.VMEM((LANES, channels), F32),
             pltpu.VMEM((TB * TB, channels), BF16),
+            pltpu.VMEM((16, TB, TB), F32),
             dma((len(operands),)),
-            dma((n_y,)),
-            dma((n_y,)),
-            dma((n_c,)),
-            dma((n_c,)),
-            dma((n_y,)),
-            dma((n_y,)),
-            dma((n_c,)),
-            dma((n_c,)),
+            *[dma((4,))] * 4,
             dma,
             dma,
             dma,
             dma((n_y,)),
             dma((n_y,)),
-            dma((5,)),
+            dma((9,)),
+            dma((4,)),
         ],
         compiler_params=pltpu.CompilerParams(
             collective_id=0, has_side_effects=True, vmem_limit_bytes=60 * 1024 * 1024

time: 51.7 us -> 47.8 us (0.925)
  Pallas kernels: 49.8 us -> 46 us
    pallas_call x1, Pallas kernels: 49.8 us -> 46 us  [shards(): pl.pallas_call(functools.partial(kernel, n_c, n_y), out_shape=jax.ShapeDt...]
where the time goes in v3:
time: 47.8 us; the launch traced here: 47.6 us
  Pallas kernels  46 us (96%)
  local copies, waits for them, and re-layouts  1.67 us (3%)
    pallas_call x1, Pallas kernels, shards(): pl.pallas_call(functools.partial(kernel, n_c, n_y), out_shape=jax.ShapeDt...  46 us
    unnamed x1, local copies, waits for them, and re-layouts  1.67 us

profile of v3, /device:TPU:1, one launch (start us, length us, event | category | flops | bytes accessed | tf_op | source)
XLA Modules:
  0.0 47.6 jit_solution(10184195091036672511)
XLA Ops:
  0.0 46.0 %shard_map.73 = f32[16,32,32]{2,1,0:T(8,128)} custom-call(bf16[128,16,128]{2,1,0:T(8,128)(2,1)} %bitcast.6, bf16[512,512]{1,0:T(8,128)(2,1)} %constant.5.filt_hbm, s32[16,128]{1,0:T(8,128)} %bitcast.7, f32[2,2048]{1,0:T(2,128)} %pos_hbm.1, f32[2,512]{1,0:T(2,128)} %dir_hbm.1, f32[2,8,2048]{2,1,0:T(8,128)} %gains_hbm.1, s32[256,512]{1,0:T(8,128)} %delays_hbm.1), custom_call_target="tpu_custom_call" | custom-call | tf_op jit(solution)/shard_map/pallas_call | solution.py:475
  46.0 1.7 %copy.10 = f32[16,32,32]{2,1,0:T(8,128)} copy(f32[16,32,32]{2,1,0:T(8,128)} %shard_map.73) | data formatting | bytes 131072

commit v4 on v3

--- a/solution.py
+++ b/solution.py
@@ -72,7 +72,7 @@
     dir_hbm,
     gains_hbm,
     delays_hbm,
-    out_hbm,
+    made_ref,
     volt_ref,
     filt_ref,
     wiring_ref,
@@ -98,7 +98,6 @@
     pow_ref,
     dm_ref,
     hot_ref,
-    made_ref,
     in_sem,
     a_send,
     a_recv,
@@ -110,7 +109,6 @@
     p_recv,
     f_send,
     own_sem,
-    out_sem,
 ):
     c = lax.axis_index("crate")
     board = lax.axis_index("board")
@@ -156,7 +154,8 @@
     loads[1].wait()
     turned = jnp.swapaxes(volt_ref[...], 0, 1)
     frame_rows = turned.shape[0] // LOCAL_ANTENNAS
-    for antenna in range(LOCAL_ANTENNAS):
+
+    def spectra(antenna):
         samples = jnp.concatenate(
             [turned[LOCAL_ANTENNAS * q + antenna] for q in range(frame_rows)], axis=1
         )
@@ -168,6 +167,9 @@
             else:
                 b_spec[antenna - 2, :, :, lanes] = jnp.swapaxes(rows[part], 0, 1).astype(BF16)
 
+    spectra(0)
+    spectra(2)
+
     def copy(src, dst, send, recv, device):
         return pltpu.make_async_remote_copy(
             src_ref=src,
@@ -209,9 +211,12 @@
         b_two.append(Exchange(b_turn.at[h], b_col.at[h], *b_sems[1], True))
 
     pl.semaphore_wait(barrier, n_y + n_c - 1)
-    for h in range(2):
-        a_one[h].start()
-        b_one[h].start()
+    a_one[0].start()
+    b_one[0].start()
+    spectra(1)
+    spectra(3)
+    a_one[1].start()
+    b_one[1].start()
 
     for load in loads[2:]:
         load.wait()
@@ -300,7 +305,10 @@
     dm_ref[...] = dot(values, moved, TN)
     mine = dm_ref[pl.ds(pl.multiple_of(board % 4 * TB, TB), TB), :]
     for d in range(TB):
-        hot_ref[d * TB : (d + 1) * TB, :] = (mine == float(d)).astype(F32).astype(BF16)
+        rows = slice(d % 8 * TB, (d % 8 + 1) * TB)
+        hot_ref[rows, d // 8 * channels : (d // 8 + 1) * channels] = (
+            (mine == float(d)).astype(F32).astype(BF16)
+        )
 
     for h in range(2):
         a_two[h].arrive()
@@ -309,8 +317,11 @@
     rows = (2 * channels, 2 * SPECTRA)
     columns = jnp.concatenate([a_col[...].reshape(rows), b_col[...].reshape(rows)], axis=0)
 
-    def beams_of(which):
-        rows = pl.ds(pl.multiple_of(which * half_beams, half_beams), half_beams)
+    chunks = half_c // n_x
+    size = half_beams // chunks
+
+    def beams_of(which, h):
+        rows = pl.ds(pl.multiple_of(which * half_beams + h * size, size), size)
         with_re = dot(wre_ref[rows, :], columns, NN)
         with_im = dot(wim_ref[rows, :], columns, NN)
         return (
@@ -318,30 +329,33 @@
             with_re[:, SPECTRA:] + with_im[:, :SPECTRA],
         )
 
-    give_re, give_im = beams_of(1 - k)
-    give_ref[0] = give_re
-    give_ref[1] = give_im
-    swap = copy(give_ref, take_ref, x_send, x_recv, partner)
-    swap.start()
-    keep_re, keep_im = beams_of(k)
-    swap.wait_recv()
-    beam_re = keep_re + take_ref[0]
-    beam_im = keep_im + take_ref[1]
-    energy = beam_re * beam_re + beam_im * beam_im
-
-    high = energy.astype(BF16)
-    low = (energy - high.astype(F32)).astype(BF16)
+    swaps = []
+    for h in range(chunks):
+        give_ref[h, 0], give_ref[h, 1] = beams_of(1 - k, h)
+        swaps.append(copy(give_ref.at[h], take_ref.at[h], x_send.at[h], x_recv.at[h], partner))
+        swaps[h].start()
+
     from_s = lax.broadcasted_iota(jnp.int32, (SPECTRA, LANES), 0)
     to_t = lax.broadcasted_iota(jnp.int32, (SPECTRA, LANES), 1)
     mean = jnp.where(from_s // AVG == to_t % TB, 1.0 / AVG, 0.0).astype(BF16)
-    power = dot(high, mean, NN) + dot(low, mean, NN)
-    beam = lax.broadcasted_iota(jnp.int32, (half_beams, LANES), 0)
-    slot = lax.broadcasted_iota(jnp.int32, (half_beams, LANES), 1)
-    power = jnp.where(beam % 4 == slot // TB, power, 0.0).astype(BF16)
-    to_row = lax.broadcasted_iota(jnp.int32, (half_beams // 4, half_beams), 0)
-    of_beam = lax.broadcasted_iota(jnp.int32, (half_beams // 4, half_beams), 1)
+    beam = lax.broadcasted_iota(jnp.int32, (size, LANES), 0)
+    slot = lax.broadcasted_iota(jnp.int32, (size, LANES), 1)
+    to_row = lax.broadcasted_iota(jnp.int32, (size // 4, size), 0)
+    of_beam = lax.broadcasted_iota(jnp.int32, (size // 4, size), 1)
     gather = (of_beam // 4 == to_row).astype(F32).astype(BF16)
-    piece_ref[...] = dot(gather, power, NN).reshape(half_c, 4, LANES).astype(BF16)
+
+    def powers(h):
+        keep_re, keep_im = beams_of(k, h)
+        swaps[h].wait_recv()
+        beam_re = keep_re + take_ref[h, 0]
+        beam_im = keep_im + take_ref[h, 1]
+        energy = beam_re * beam_re + beam_im * beam_im
+        high = energy.astype(BF16)
+        low = (energy - high.astype(F32)).astype(BF16)
+        power = dot(high, mean, NN) + dot(low, mean, NN)
+        power = jnp.where(beam % 4 == slot // TB, power, 0.0).astype(BF16)
+        rows = dot(gather, power, NN).reshape(n_x, 4, LANES)
+        piece_ref[h * n_x : (h + 1) * n_x] = rows.astype(BF16)
 
     holds = c // half_c == k
     count = half_c * n_y
@@ -355,15 +369,17 @@
             (k * half_c + index, 2 * to_y + k),
         )
 
-    indices = [h * n_x + (x + dx) % n_x for dx in far_first(n_x) for h in range(half_c // n_x)]
-    for to_y in places:
+    for h in range(chunks):
+        powers(h)
+        indices = [h * n_x + (x + dx) % n_x for dx in far_first(n_x)]
+        for to_y in places:
+            for index in indices:
+                p_copy(index, to_y).start()
         for index in indices:
-            p_copy(index, to_y).start()
-    for index in indices:
-
-        @pl.when(k * half_c + index != c)
-        def _():
-            p_copy(index, y).start()
+
+            @pl.when(k * half_c + index != c)
+            def _():
+                p_copy(index, y).start()
 
     def group(source, size):
         return pow_ref.at[pl.ds(pl.multiple_of(source * n_c, n_c), size)]
@@ -403,38 +419,47 @@
         lax.fori_loop(0, n_y, f_wait, 0)
 
     series = jnp.swapaxes(pow_ref[...].reshape(tiles, 16, LANES), 0, 1)
-
-    def put(first):
-        rows = pl.ds(first, 4)
-        return pltpu.make_async_copy(made_ref.at[rows], out_hbm.at[rows], out_sem.at[first // 4])
-
+    flat = series.reshape(16 * tiles, LANES)
+    source = lax.broadcasted_iota(jnp.int32, (LANES, LANES), 0)
+    place = lax.broadcasted_iota(jnp.int32, (LANES, LANES), 1)
+
+    def shift(n):
+        chosen = source == place // TB * TB + (place + 8 * n) % TB
+        return chosen.astype(F32).astype(BF16)
+
+    near = dot(flat, jnp.concatenate([shift(1), shift(2)], axis=1), NN).astype(BF16)
+    shifted = [flat, near[:, :LANES], near[:, LANES:], dot(flat, shift(3), NN).astype(BF16)]
+    shifted = [v.reshape(16, tiles, LANES) for v in shifted]
     for pair in range(2):
         both = [
-            jnp.concatenate([series[4 * r + 2 * pair + j] for r in range(4)], axis=0)
+            jnp.concatenate([v[4 * r + 2 * pair + j] for v in shifted for r in range(4)], axis=0)
             for j in range(2)
         ]
         sums = dot(hot_ref[...], jnp.concatenate(both, axis=1), NN)
+        mean_of = []
+        for j in range(2):
+            level = dot(jnp.ones((8, channels), BF16), both[j][:channels], NN)
+            step = TB // 2
+            while step:
+                level = level + rotate(level, step)
+                step //= 2
+            mean_of.append(level[:1] * (1.0 / TB))
         for j in range(2):
             total = sums[:, j * LANES : (j + 1) * LANES]
-            step = TB // 2
+            step = 4
             while step:
                 rows = step * TB
                 total = total[:rows] + rotate(total[rows:], step)
                 step //= 2
-            mean_of = total
-            step = TB // 2
-            while step:
-                mean_of = mean_of + rotate(mean_of, step)
-                step //= 2
-            result = (total - mean_of * (1.0 / TB)) * (1.0 / math.sqrt(channels))
+            result = (total - mean_of[j]) * (1.0 / math.sqrt(channels))
             first = 4 * (2 * pair + j)
             for q in range(4):
                 made_ref[first + q] = result[:, q * TB : (q + 1) * TB]
-            put(first).start()
 
     for one in a_one + a_two + b_one + b_two:
         one.all.wait_send()
-    swap.wait_send()
+    for swap in swaps:
+        swap.wait_send()
 
     @pl.when(holds)
     def _():
@@ -451,9 +476,6 @@
     def _():
         rows = pow_ref.at[pl.ds(0, count)]
         copy(rows, rows, p_send, p_recv.at[0], partner).wait_send()
-
-    for first in range(0, 16, 4):
-        put(first).wait()
 
 
 def shards(n_c, n_y, voltages, wiring, positions, directions, gains, delays):
@@ -462,6 +484,7 @@
     plane = 4 * channels
     beams = 16 * n_c
     half_beams = beams // 2
+    chunks = n_c // 2 // min(8, n_c)
     samples = voltages.reshape(LOCAL_ANTENNAS, SPECTRA * frame // LANES, LANES).transpose(1, 0, 2)
     samples = samples.reshape(SPECTRA, frame // LANES * LOCAL_ANTENNAS, LANES)
     table = filter_rows(channels, n_c, n_y)
@@ -474,9 +497,9 @@
     by_c = pltpu.VMEM((2, n_c, n_y, 2 * SPECTRA), BF16)
     return pl.pallas_call(
         functools.partial(kernel, n_c, n_y),
-        out_shape=jax.ShapeDtypeStruct((16, TB, TB), F32),
+        out_shape=pltpu.VMEM((16, TB, TB), F32),
         in_specs=[pl.BlockSpec(memory_space=pl.ANY)] * len(operands),
-        out_specs=pl.BlockSpec(memory_space=pl.ANY),
+        out_specs=pl.BlockSpec(memory_space=pltpu.VMEM),
         scratch_shapes=[
             *loaded,
             *[by_y, by_y, by_c, by_c],
@@ -485,22 +508,18 @@
             pltpu.VMEM((2, beams, LANES), F32),
             pltpu.VMEM((beams, plane), BF16),
             pltpu.VMEM((beams, plane), BF16),
-            pltpu.VMEM((2, half_beams, SPECTRA), F32),
-            pltpu.VMEM((2, half_beams, SPECTRA), F32),
+            *[pltpu.VMEM((chunks, 2, half_beams // chunks, SPECTRA), F32)] * 2,
             pltpu.VMEM((n_c // 2, 4, LANES), BF16),
             pltpu.VMEM((channels, 4, LANES), BF16),
             pltpu.VMEM((LANES, channels), F32),
-            pltpu.VMEM((TB * TB, channels), BF16),
-            pltpu.VMEM((16, TB, TB), F32),
+            pltpu.VMEM((8 * TB, 4 * channels), BF16),
             dma((len(operands),)),
             *[dma((4,))] * 4,
-            dma,
-            dma,
+            *[dma((chunks,))] * 2,
             dma,
             dma((n_y,)),
             dma((n_y,)),
             dma((9,)),
-            dma((4,)),
         ],
         compiler_params=pltpu.CompilerParams(
             collective_id=0, has_side_effects=True, vmem_limit_bytes=60 * 1024 * 1024

time: 47.8 us -> 45.1 us (0.944)
  Pallas kernels: 46 us -> 44.2 us
  local copies, waits for them, and re-layouts: 1.67 us -> 0.71 us
    pallas_call x1, Pallas kernels: 46 us -> 44.2 us  [shards(): pl.pallas_call(functools.partial(kernel, n_c, n_y), out_shape=pltpu.VMEM(...]
    unnamed x1, local copies, waits for them, and re-layouts: 1.67 us -> 0.71 us
where the time goes in v4:
time: 45.1 us; the launch traced here: 44.9 us
  Pallas kernels  44.2 us (98%)
  local copies, waits for them, and re-layouts  0.71 us (2%)
    pallas_call x1, Pallas kernels, shards(): pl.pallas_call(functools.partial(kernel, n_c, n_y), out_shape=pltpu.VMEM(...  44.2 us

profile of v4, /device:TPU:1, one launch (start us, length us, event | category | flops | bytes accessed | tf_op | source)
XLA Modules:
  0.0 44.9 jit_solution(16809114097427294709)
XLA Ops:
  0.0 44.2 %shard_map.73 = f32[16,32,32]{2,1,0:T(8,128)S(1)} custom-call(bf16[128,16,128]{2,1,0:T(8,128)(2,1)} %bitcast.6, bf16[512,512]{1,0:T(8,128)(2,1)} %constant.5.filt_hbm, s32[16,128]{1,0:T(8,128)} %bitcast.7, f32[2,2048]{1,0:T(2,128)} %pos_hbm.1, f32[2,512]{1,0:T(2,128)} %dir_hbm.1, f32[2,8,2048]{2,1,0:T(8,128)} %gains_hbm.1, s32[256,512]{1,0:T(8,128)} %delays_hbm.1), custom_call_target="tpu_custom_call" | custom-call | tf_op jit(solution)/shard_map/pallas_call | solution.py:498
  44.2 0.7 %copy.10 = f32[16,32,32]{2,1,0:T(8,128)} copy(f32[16,32,32]{2,1,0:T(8,128)S(1)} %shard_map.73) | data formatting | bytes 131072

commit v5 on v4

--- a/solution.py
+++ b/solution.py
@@ -13,6 +13,7 @@
 TB = 32
 LOCAL_ANTENNAS = 4
 SPECTRA = 128
+SIZE_X = 4
 LANES = 128
 ROWS = 64
 MESH = pl.DeviceIdType.MESH
@@ -40,11 +41,15 @@
     frame = 2 * channels
     sample = np.arange(frame)
     window = 0.5 - 0.5 * np.cos(2 * np.pi / frame * sample)
-    channel = (np.arange(n_c)[None, :] * n_y + np.arange(n_y)[:, None]).reshape(-1)
-    angle = 2 * np.pi / frame * (channel[:, None] * sample[None, :] % frame)
+    by_y = np.arange(n_c)[None, :] * n_y + np.arange(n_y)[:, None]
+    by_z = by_y.reshape(n_y, -1, SIZE_X).transpose(1, 0, 2)
     scale = 1.0 / math.sqrt(3.0 * frame / 8.0)
-    table = np.concatenate([np.cos(angle), -np.sin(angle)], axis=0) * window[None, :] * scale
-    return jnp.asarray(table.astype(np.float32)).astype(BF16)
+    tables = []
+    for channel in (by_y.reshape(-1), by_z.reshape(-1)):
+        angle = 2 * np.pi / frame * (channel[:, None] * sample[None, :] % frame)
+        table = np.concatenate([np.cos(angle), -np.sin(angle)], axis=0)
+        tables.append(table * window[None, :] * scale)
+    return jnp.asarray(np.stack(tables).astype(np.float32)).astype(BF16)
 
 
 def far_first(size):
@@ -121,7 +126,7 @@
     half_beams = beams // 2
     half_c = n_c // 2
     partner = (c, 2 * y + 1 - k)
-    n_x = min(8, n_c)
+    n_x = SIZE_X
     n_z = n_c // n_x
     x = c % n_x
     z = c // n_x
@@ -131,6 +136,11 @@
     steps_c.sort(key=lambda s: -min(s[0], n_z - s[0]) - min(s[1], n_x - s[1]))
     crates = [(z + dz) % n_z * n_x + (x + dx) % n_x for dz, dx in steps_c[:-1]]
     places = [(y + dy) % n_y for dy in far_first(n_y)[:-1]]
+    places_z = [(z + dz) % n_z for dz in far_first(n_z)[:-1]]
+    places_x = [(x + dx) % n_x for dx in far_first(n_x)[:-1]]
+    steps_yx = [(dy, dx) for dy in range(n_y) for dx in range(n_x)]
+    steps_yx.sort(key=lambda s: -min(s[0], n_y - s[0]) - min(s[1], n_x - s[1]))
+    places_yx = [(y + dy) % n_y * n_x + (x + dx) % n_x for dy, dx in steps_yx[:-1]]
 
     offset = pl.multiple_of(board // 4 * LANES, LANES)
     pairs = [
@@ -147,7 +157,9 @@
         load.start()
 
     barrier = pltpu.get_barrier_semaphore()
-    for device in [(i, board) for i in crates] + [(c, 2 * i + k) for i in places] + [partner]:
+    near_ones = [(c, 2 * i + k) for i in places] + [(z * n_x + i, board) for i in places_x]
+    near_ones += [(i * n_x + x, board) for i in places_z] + [partner]
+    for device in near_ones:
         pl.semaphore_signal(barrier, inc=1, device_id=device, device_id_type=MESH)
 
     loads[0].wait()
@@ -159,13 +171,11 @@
         samples = jnp.concatenate(
             [turned[LOCAL_ANTENNAS * q + antenna] for q in range(frame_rows)], axis=1
         )
-        rows = dot(filt_ref[...], samples, NT).reshape(2, n_y, n_c, SPECTRA)
+        rows = dot(filt_ref[antenna // 2], samples, NT)
+        first, spec_ref = ((n_y, a_spec), (n_z, b_spec))[antenna // 2]
+        rows = rows.reshape(2, first, channels // first, SPECTRA).astype(BF16)
         for part in range(2):
-            lanes = slice(part * SPECTRA, (part + 1) * SPECTRA)
-            if antenna < 2:
-                a_spec[antenna, :, :, lanes] = rows[part].astype(BF16)
-            else:
-                b_spec[antenna - 2, :, :, lanes] = jnp.swapaxes(rows[part], 0, 1).astype(BF16)
+            spec_ref[antenna % 2, :, :, part * SPECTRA : (part + 1) * SPECTRA] = rows[part]
 
     spectra(0)
     spectra(2)
@@ -181,11 +191,10 @@
         )
 
     class Exchange:
-        def __init__(self, src, dst, send, recv, own_sem, along_y):
+        def __init__(self, src, dst, send, recv, own_sem, along):
             self.refs = (src, dst)
             self.sems = (send, recv)
-            self.here, self.others = (y, places) if along_y else (c, crates)
-            self.device = (lambda i: (c, 2 * i + k)) if along_y else (lambda i: (i, board))
+            self.here, self.others, self.device = along
             own = (src.at[self.here], dst.at[self.here], own_sem)
             self.own = pltpu.make_async_copy(*own)
             count = pl.ds(0, len(self.others))
@@ -201,16 +210,20 @@
             self.own.wait()
             self.all.wait_recv()
 
+    along_y = (y, places, lambda i: (c, 2 * i + k))
+    over_c = (c, crates, lambda i: (i, board))
+    along_z = (z, places_z, lambda i: (i * n_x + x, board))
+    over_yx = (y * n_x + x, places_yx, lambda i: (z * n_x + i % n_x, i // n_x * 2 + k))
     a_one, a_two, b_one, b_two = [], [], [], []
     for h in range(2):
         a_sems = [(a_send.at[s], a_recv.at[s], own_sem.at[s]) for s in (h, 2 + h)]
         b_sems = [(b_send.at[s], b_recv.at[s], own_sem.at[4 + s]) for s in (h, 2 + h)]
-        a_one.append(Exchange(a_spec.at[h], a_got.at[h], *a_sems[0], True))
-        a_two.append(Exchange(a_turn.at[h], a_col.at[h], *a_sems[1], False))
-        b_one.append(Exchange(b_spec.at[h], b_got.at[h], *b_sems[0], False))
-        b_two.append(Exchange(b_turn.at[h], b_col.at[h], *b_sems[1], True))
-
-    pl.semaphore_wait(barrier, n_y + n_c - 1)
+        a_one.append(Exchange(a_spec.at[h], a_got.at[h], *a_sems[0], along_y))
+        a_two.append(Exchange(a_turn.at[h], a_col.at[h], *a_sems[1], over_c))
+        b_one.append(Exchange(b_spec.at[h], b_got.at[h], *b_sems[0], along_z))
+        b_two.append(Exchange(b_turn.at[h], b_col.at[h], *b_sems[1], over_yx))
+
+    pl.semaphore_wait(barrier, len(near_ones))
     a_one[0].start()
     b_one[0].start()
     spectra(1)
@@ -226,7 +239,8 @@
     antenna = place // channels
     device = place % channels
     of_a = device // n_y * 2 * n_y + device % n_y * 2 + k
-    of_b = device % n_c * 2 * n_y + device // n_c * 2 + k
+    crate = device % n_z * n_x + device % n_c // n_z
+    of_b = crate * 2 * n_y + device // n_c * 2 + k
     row_id = jnp.where(antenna < 2, of_a, of_b) * 4 + antenna
 
     def look_up(index, row_of, dtype):
@@ -290,8 +304,8 @@
     for h in range(2):
         a_one[h].arrive()
         a_turn[h] = jnp.swapaxes(a_got[h], 0, 1)
+        b_one[h].arrive()
         a_two[h].start()
-        b_one[h].arrive()
         b_turn[h] = jnp.swapaxes(b_got[h], 0, 1)
         b_two[h].start()
     lax.fori_loop(steps // 2, steps, weights_block, 0)
@@ -317,8 +331,9 @@
     rows = (2 * channels, 2 * SPECTRA)
     columns = jnp.concatenate([a_col[...].reshape(rows), b_col[...].reshape(rows)], axis=0)
 
-    chunks = half_c // n_x
+    chunks = 2
     size = half_beams // chunks
+    served = half_c // chunks
 
     def beams_of(which, h):
         rows = pl.ds(pl.multiple_of(which * half_beams + h * size, size), size)
@@ -344,8 +359,10 @@
     of_beam = lax.broadcasted_iota(jnp.int32, (size // 4, size), 1)
     gather = (of_beam // 4 == to_row).astype(F32).astype(BF16)
 
+    kept = [beams_of(k, h) for h in range(chunks)]
+
     def powers(h):
-        keep_re, keep_im = beams_of(k, h)
+        keep_re, keep_im = kept[h]
         swaps[h].wait_recv()
         beam_re = keep_re + take_ref[h, 0]
         beam_im = keep_im + take_ref[h, 1]
@@ -354,8 +371,8 @@
         low = (energy - high.astype(F32)).astype(BF16)
         power = dot(high, mean, NN) + dot(low, mean, NN)
         power = jnp.where(beam % 4 == slot // TB, power, 0.0).astype(BF16)
-        rows = dot(gather, power, NN).reshape(n_x, 4, LANES)
-        piece_ref[h * n_x : (h + 1) * n_x] = rows.astype(BF16)
+        rows = dot(gather, power, NN).reshape(served, 4, LANES)
+        piece_ref[h * served : (h + 1) * served] = rows.astype(BF16)
 
     holds = c // half_c == k
     count = half_c * n_y
@@ -371,7 +388,8 @@
 
     for h in range(chunks):
         powers(h)
-        indices = [h * n_x + (x + dx) % n_x for dx in far_first(n_x)]
+        tails = [h * served + (x + dx) % n_x for dx in far_first(n_x)]
+        indices = [i + tail for tail in tails for i in range(0, served, n_x)]
         for to_y in places:
             for index in indices:
                 p_copy(index, to_y).start()
@@ -484,7 +502,6 @@
     plane = 4 * channels
     beams = 16 * n_c
     half_beams = beams // 2
-    chunks = n_c // 2 // min(8, n_c)
     samples = voltages.reshape(LOCAL_ANTENNAS, SPECTRA * frame // LANES, LANES).transpose(1, 0, 2)
     samples = samples.reshape(SPECTRA, frame // LANES * LOCAL_ANTENNAS, LANES)
     table = filter_rows(channels, n_c, n_y)
@@ -495,6 +512,10 @@
     dma = pltpu.SemaphoreType.DMA
     by_y = pltpu.VMEM((2, n_y, n_c, 2 * SPECTRA), BF16)
     by_c = pltpu.VMEM((2, n_c, n_y, 2 * SPECTRA), BF16)
+    n_z = n_c // SIZE_X
+    chunks = 2
+    by_z = pltpu.VMEM((2, n_z, channels // n_z, 2 * SPECTRA), BF16)
+    by_yx = pltpu.VMEM((2, channels // n_z, n_z, 2 * SPECTRA), BF16)
     return pl.pallas_call(
         functools.partial(kernel, n_c, n_y),
         out_shape=pltpu.VMEM((16, TB, TB), F32),
@@ -503,7 +524,7 @@
         scratch_shapes=[
             *loaded,
             *[by_y, by_y, by_c, by_c],
-            *[by_c, by_c, by_y, by_y],
+            *[by_z, by_z, by_yx, by_yx],
             pltpu.VMEM((6, plane // LANES, LANES), F32),
             pltpu.VMEM((2, beams, LANES), F32),
             pltpu.VMEM((beams, plane), BF16),

time: 45.1 us -> 44 us (0.976)
  Pallas kernels: 44.2 us -> 43.1 us
    pallas_call x1, Pallas kernels: 44.2 us -> 43.1 us  [shards(): pl.pallas_call(functools.partial(kernel, n_c, n_y), out_shape=pltpu.VMEM(...]
where the time goes in v5:
time: 44 us; the launch traced here: 43.8 us
  Pallas kernels  43.1 us (98%)
  local copies, waits for them, and re-layouts  0.71 us (2%)
    pallas_call x1, Pallas kernels, shards(): pl.pallas_call(functools.partial(kernel, n_c, n_y), out_shape=pltpu.VMEM(...  43.1 us

profile of v5, /device:TPU:1, one launch (start us, length us, event | category | flops | bytes accessed | tf_op | source)
XLA Modules:
  0.0 43.8 jit_solution(4143500770087479592)
XLA Ops:
  0.0 43.1 %shard_map.73 = f32[16,32,32]{2,1,0:T(8,128)S(1)} custom-call(bf16[128,16,128]{2,1,0:T(8,128)(2,1)} %bitcast.6, bf16[2,512,512]{2,1,0:T(8,128)(2,1)} %constant.5.filt_hbm, s32[16,128]{1,0:T(8,128)} %bitcast.7, f32[2,2048]{1,0:T(2,128)} %pos_hbm.1, f32[2,512]{1,0:T(2,128)} %dir_hbm.1, f32[2,8,2048]{2,1,0:T(8,128)} %gains_hbm.1, s32[256,512]{1,0:T(8,128)} %delays_hbm.1), custom_call_target="tpu_custom_call" | custom-call | tf_op jit(solution)/shard_map/pallas_call | solution.py:519
  43.1 0.7 %copy.10 = f32[16,32,32]{2,1,0:T(8,128)} copy(f32[16,32,32]{2,1,0:T(8,128)S(1)} %shard_map.73) | data formatting | bytes 131072

commit v6 on v5

--- a/solution.py
+++ b/solution.py
@@ -62,9 +62,8 @@
 
 def rotate(x, k):
     lane = lax.broadcasted_iota(jnp.int32, x.shape, x.ndim - 1)
-    return jnp.take_along_axis(
-        x, lane // TB * TB + (lane + k) % TB, axis=x.ndim - 1, mode="promise_in_bounds"
-    )
+    index = (lane & ~(TB - 1)) | ((lane + k) & (TB - 1))
+    return jnp.take_along_axis(x, index, axis=x.ndim - 1, mode="promise_in_bounds")
 
 
 def kernel(
@@ -103,6 +102,10 @@
     pow_ref,
     dm_ref,
     hot_ref,
+    mean_ref,
+    four_ref,
+    gather_ref,
+    shift_ref,
     in_sem,
     a_send,
     a_recv,
@@ -324,16 +327,31 @@
             (mine == float(d)).astype(F32).astype(BF16)
         )
 
+    chunks = 2
+    size = half_beams // chunks
+    served = half_c // chunks
+
+    from_s = lax.broadcasted_iota(jnp.int32, (SPECTRA, LANES), 0)
+    to_t = lax.broadcasted_iota(jnp.int32, (SPECTRA, LANES), 1)
+    mean = jnp.where(from_s // AVG == to_t % TB, 1.0 / AVG, 0.0).astype(BF16)
+    beam = lax.broadcasted_iota(jnp.int32, (size, LANES), 0)
+    slot = lax.broadcasted_iota(jnp.int32, (size, LANES), 1)
+    to_row = lax.broadcasted_iota(jnp.int32, (size // 4, size), 0)
+    of_beam = lax.broadcasted_iota(jnp.int32, (size // 4, size), 1)
+    gather = (of_beam // 4 == to_row).astype(F32).astype(BF16)
+    mean_ref[...] = mean
+    four_ref[...] = jnp.where(beam % 4 == slot // TB, 1.0, 0.0)
+    gather_ref[...] = gather
+    for n in range(3):
+        chosen = from_s == to_t // TB * TB + (to_t + 8 * n + 8) % TB
+        shift_ref[:, n * LANES : (n + 1) * LANES] = chosen.astype(F32).astype(BF16)
+
     for h in range(2):
         a_two[h].arrive()
         b_two[h].arrive()
 
     rows = (2 * channels, 2 * SPECTRA)
     columns = jnp.concatenate([a_col[...].reshape(rows), b_col[...].reshape(rows)], axis=0)
-
-    chunks = 2
-    size = half_beams // chunks
-    served = half_c // chunks
 
     def beams_of(which, h):
         rows = pl.ds(pl.multiple_of(which * half_beams + h * size, size), size)
@@ -350,15 +368,6 @@
         swaps.append(copy(give_ref.at[h], take_ref.at[h], x_send.at[h], x_recv.at[h], partner))
         swaps[h].start()
 
-    from_s = lax.broadcasted_iota(jnp.int32, (SPECTRA, LANES), 0)
-    to_t = lax.broadcasted_iota(jnp.int32, (SPECTRA, LANES), 1)
-    mean = jnp.where(from_s // AVG == to_t % TB, 1.0 / AVG, 0.0).astype(BF16)
-    beam = lax.broadcasted_iota(jnp.int32, (size, LANES), 0)
-    slot = lax.broadcasted_iota(jnp.int32, (size, LANES), 1)
-    to_row = lax.broadcasted_iota(jnp.int32, (size // 4, size), 0)
-    of_beam = lax.broadcasted_iota(jnp.int32, (size // 4, size), 1)
-    gather = (of_beam // 4 == to_row).astype(F32).astype(BF16)
-
     kept = [beams_of(k, h) for h in range(chunks)]
 
     def powers(h):
@@ -369,9 +378,9 @@
         energy = beam_re * beam_re + beam_im * beam_im
         high = energy.astype(BF16)
         low = (energy - high.astype(F32)).astype(BF16)
-        power = dot(high, mean, NN) + dot(low, mean, NN)
-        power = jnp.where(beam % 4 == slot // TB, power, 0.0).astype(BF16)
-        rows = dot(gather, power, NN).reshape(served, 4, LANES)
+        power = dot(high, mean_ref[...], NN) + dot(low, mean_ref[...], NN)
+        power = jnp.where(four_ref[...] > 0.0, power, 0.0).astype(BF16)
+        rows = dot(gather_ref[...], power, NN).reshape(served, 4, LANES)
         piece_ref[h * served : (h + 1) * served] = rows.astype(BF16)
 
     holds = c // half_c == k
@@ -438,15 +447,8 @@
 
     series = jnp.swapaxes(pow_ref[...].reshape(tiles, 16, LANES), 0, 1)
     flat = series.reshape(16 * tiles, LANES)
-    source = lax.broadcasted_iota(jnp.int32, (LANES, LANES), 0)
-    place = lax.broadcasted_iota(jnp.int32, (LANES, LANES), 1)
-
-    def shift(n):
-        chosen = source == place // TB * TB + (place + 8 * n) % TB
-        return chosen.astype(F32).astype(BF16)
-
-    near = dot(flat, jnp.concatenate([shift(1), shift(2)], axis=1), NN).astype(BF16)
-    shifted = [flat, near[:, :LANES], near[:, LANES:], dot(flat, shift(3), NN).astype(BF16)]
+    near = dot(flat, shift_ref[:, : 2 * LANES], NN).astype(BF16)
+    shifted = [flat, near[:, :LANES], near[:, LANES:], dot(flat, shift_ref[:, 2 * LANES :], NN).astype(BF16)]
     shifted = [v.reshape(16, tiles, LANES) for v in shifted]
     for pair in range(2):
         both = [
@@ -534,6 +536,10 @@
             pltpu.VMEM((channels, 4, LANES), BF16),
             pltpu.VMEM((LANES, channels), F32),
             pltpu.VMEM((8 * TB, 4 * channels), BF16),
+            pltpu.VMEM((SPECTRA, LANES), BF16),
+            pltpu.VMEM((half_beams // chunks, LANES), F32),
+            pltpu.VMEM((half_beams // chunks // 4, half_beams // chunks), BF16),
+            pltpu.VMEM((LANES, 3 * LANES), BF16),
             dma((len(operands),)),
             *[dma((4,))] * 4,
             *[dma((chunks,))] * 2,

time: 44 us -> 43.9 us (level)
  no operation moved by 1% of the time
where the time goes in v6:
time: 43.9 us; the launch traced here: 43.8 us
  Pallas kernels  43.1 us (98%)
  local copies, waits for them, and re-layouts  0.71 us (2%)
    pallas_call x1, Pallas kernels, shards(): pl.pallas_call(functools.partial(kernel, n_c, n_y), out_shape=pltpu.VMEM(...  43.1 us

profile of v6, /device:TPU:1, one launch (start us, length us, event | category | flops | bytes accessed | tf_op | source)
XLA Modules:
  0.0 43.8 jit_solution(17200581984058480145)
XLA Ops:
  0.0 43.1 %shard_map.73 = f32[16,32,32]{2,1,0:T(8,128)S(1)} custom-call(bf16[128,16,128]{2,1,0:T(8,128)(2,1)} %bitcast.6, bf16[2,512,512]{2,1,0:T(8,128)(2,1)} %constant.5.filt_hbm, s32[16,128]{1,0:T(8,128)} %bitcast.7, f32[2,2048]{1,0:T(2,128)} %pos_hbm.1, f32[2,512]{1,0:T(2,128)} %dir_hbm.1, f32[2,8,2048]{2,1,0:T(8,128)} %gains_hbm.1, s32[256,512]{1,0:T(8,128)} %delays_hbm.1), custom_call_target="tpu_custom_call" | custom-call | tf_op jit(solution)/shard_map/pallas_call | solution.py:521
  43.1 0.7 %copy.10 = f32[16,32,32]{2,1,0:T(8,128)} copy(f32[16,32,32]{2,1,0:T(8,128)S(1)} %shard_map.73) | data formatting | bytes 131072
